TPU v7x, 32 devices: a whole 2x2x4 slice. The times are simulated.
32 devices in a mesh: groups: 2 (over x), dom: 16 (over z, y, core).
Axes of the slice: x: 2, y: 2, z: 4, core: 2. Of those that a mesh axis runs over, the one named last changes fastest.
Arguments:
- particle_places: float32 [16, 3, 3072], P('groups', None, 'dom'), parts along dimension 0, may hold values from 0 to 48, as said below
- particle_speeds: float32 [16, 3, 3072], P('groups', None, 'dom'), parts along dimension 0, may hold values from -7 to 7
- thermal_targets: float32 [16], P('groups'), parts along dimension 0, may hold values from 0.5 to 2
- element_features: bfloat16 [6144, 128], P(('groups', 'dom')), parts along dimension 0, may hold values from -4 to 4
- swap_counterpart_slot: int32 [16], P('groups'), parts along dimension 0, may hold values from 0 to 7, as said below
- swap_approval_flags: int32 [16], P('groups'), parts along dimension 0, may hold values from 0 to 1, as said below
- initial_signal_projector: bfloat16 [128, 128], replicated, may hold values from -0.5 to 0.5
- initial_distance_filter: float32 [8, 128], replicated, may hold values from -2 to 2
- initial_directional_scales: float32 [128], replicated, may hold values from 0.5 to 1.5
- invariant_revision_matrix: bfloat16 [128, 128], replicated, may hold values from -0.5 to 0.5
- magnitude_revision_matrix: bfloat16 [128, 128], replicated, may hold values from -0.5 to 0.5
- later_signal_projector: bfloat16 [128, 128], replicated, may hold values from -0.5 to 0.5
- later_directional_scales: float32 [128], replicated, may hold values from 0.5 to 1.5
- push_output_matrix: float32 [128], replicated, may hold values from -0.5 to 0.5
Outputs:
- positions_new: float32 [16, 3, 3072], P('groups', None, 'dom'), parts along dimension 0
- velocities_new: float32 [16, 3, 3072], P('groups', None, 'dom'), parts along dimension 0
- forces_new: float32 [16, 3, 3072], P('groups', None, 'dom'), parts along dimension 0
There are 2 independent parts, one for each index of `groups`. A program takes and returns all parts, laid end to end along the dimension named above; an argument that names none is the same for every part. Nothing has to cross between parts.
Inputs may be any that keep to these rules, and one draw needn't show every extreme that they name: `particle_places`: the atoms of cell k have x and y in [0, 1) and z in [k, k + 1). `swap_counterpart_slot`: an involution that pairs neighbouring replicas, either (0, 1), (2, 3), ... or (1, 2), (3, 4), ..., a replica left without a pair being its own partner. `swap_approval_flags`: equal for the two replicas of a pair, 0 for a replica that is its own partner.
All inputs are finite; a program needn't handle non-finite values.
Results may differ from a plain program's by a relative error of at most 0.012.
The roundings to bfloat16 on the way count: a program that leaves them out, or rounds other values in their place, can miss the bound.
Values may be sent and summed in bfloat16 or wider, within the bound.
A program may use at most 64 MiB of HBM per device.

v0:
```python
import jax
import jax.numpy as jnp
from jax import lax
from jax.sharding import PartitionSpec as P

NA = 64
HC = 1
STEPS = 4


step_time = 0.05
motion_work_lower_limit = 1e-06


def with_halo(cells, sides, width):
    for axis, dim in sides:
        count = lax.axis_size(axis)
        head = lax.slice_in_dim(cells, 0, width, axis=dim)
        tail = lax.slice_in_dim(cells, cells.shape[dim] - width, cells.shape[dim], axis=dim)
        cells = jnp.concatenate(
            [
                lax.ppermute(tail, axis, [(i, (i + 1) % count) for i in range(count)]),
                cells,
                lax.ppermute(head, axis, [((i + 1) % count, i) for i in range(count)]),
            ],
            axis=dim,
        )
    return cells


def radial_rows(own_coords, part_coords, basis_count):
    displacement = part_coords[:, :, :, None, :] - own_coords[:, :, :, :, None]
    squared = jnp.sum(displacement * displacement, axis=1)
    envelope = jnp.where(squared < 1.0, (1.0 - squared) * (1.0 - squared), 0.0)
    vectors = jnp.moveaxis(displacement * envelope[:, None], 1, 3)
    if basis_count == 0:
        return vectors.astype(jnp.bfloat16)
    centers = jnp.arange(basis_count, dtype=jnp.float32) / (basis_count - 1)
    sharpness = 2.0 * (basis_count - 1) * (basis_count - 1)
    offset = squared[:, :, :, None, :] - centers[:, None]
    gaussians = jnp.exp(-sharpness * offset * offset) * envelope[:, :, :, None, :]
    return jnp.concatenate([gaussians, vectors], axis=3).astype(jnp.bfloat16)


def coord_windows(location_triples, first_cell, cell_count):
    leading = location_triples.shape[:2]
    own_coords = location_triples[:, :, first_cell * NA : (first_cell + cell_count) * NA].reshape(
        leading + (cell_count, NA)
    )
    pieces = []
    for neighbor in range(2 * HC + 1):
        begin_atom = (first_cell - HC + neighbor) * NA
        pieces.append(
            location_triples[:, :, begin_atom : begin_atom + cell_count * NA].reshape(
                leading + (cell_count, NA)
            )
        )
    return (own_coords, jnp.concatenate(pieces, axis=3))


def feature_windows(features, first_cell, cell_count):
    leading = features.shape[:-2]
    channels = features.shape[-1]
    pieces = []
    for neighbor in range(2 * HC + 1):
        begin_atom = (first_cell - HC + neighbor) * NA
        pieces.append(
            features[..., begin_atom : begin_atom + cell_count * NA, :].reshape(
                leading + (cell_count, NA, channels)
            )
        )
    return jnp.concatenate(pieces, axis=-2)


def periodic_shift(extended, halo_cells):
    own_index = lax.axis_index("dom")
    local_cells = extended.shape[2] // NA - 2 * halo_cells
    total_cells = local_cells * lax.axis_size("dom")
    cell_number = (
        own_index * local_cells - halo_cells + jnp.arange(extended.shape[2], dtype=jnp.int32) // NA
    )
    wrap_shift = (
        jnp.where(cell_number < 0, -1.0, 0.0) + jnp.where(cell_number >= total_cells, 1.0, 0.0)
    ) * total_cells
    axis_mask = jnp.array([0.0, 0.0, 1.0], jnp.float32)
    return extended + axis_mask[None, :, None] * wrap_shift[None, None, :]


def layer_one(
    location_triples,
    first_cell,
    cell_count,
    first_table,
    self_rows,
    initial_distance_filter,
    initial_directional_scales,
    invariant_revision_matrix,
    magnitude_revision_matrix,
):
    replicas = location_triples.shape[0]
    channels = invariant_revision_matrix.shape[0]
    basis_count = initial_distance_filter.shape[0]
    own_coords, part_coords = coord_windows(location_triples, first_cell, cell_count)
    single_row_count = radial_rows(own_coords, part_coords, basis_count)
    exchange_mate = feature_windows(first_table, first_cell, cell_count)
    reduced_sum = jnp.einsum(
        "vyegd,ydm->vyegm", single_row_count, exchange_mate, preferred_element_type=jnp.float32
    )
    scalar = jnp.sum(reduced_sum[:, :, :, :basis_count] * initial_distance_filter, axis=3)
    vector_one = reduced_sum[:, :, :, basis_count:] * initial_directional_scales
    norm_square = jnp.sum(vector_one * vector_one, axis=3)
    update = jnp.dot(
        scalar.astype(jnp.bfloat16).reshape(-1, channels),
        invariant_revision_matrix,
        preferred_element_type=jnp.float32,
    )
    update = update + jnp.dot(
        norm_square.astype(jnp.bfloat16).reshape(-1, channels),
        magnitude_revision_matrix,
        preferred_element_type=jnp.float32,
    )
    hidden = self_rows.astype(jnp.float32)[None] + jax.nn.silu(update).reshape(
        replicas, cell_count * NA, channels
    )
    return (hidden.astype(jnp.bfloat16), vector_one)


def layer_two(location_triples, first_cell, cell_count, second_table, later_directional_scales):
    own_coords, part_coords = coord_windows(location_triples, first_cell, cell_count)
    rows_two = radial_rows(own_coords, part_coords, 0)
    exchange_mate = feature_windows(second_table, first_cell, cell_count)
    reduced_sum = jnp.einsum(
        "rcaxb,rcbf->rcaxf", rows_two, exchange_mate, preferred_element_type=jnp.float32
    )
    return reduced_sum * later_directional_scales


def readout(vectors, push_output_matrix):
    reduced_sum = jnp.sum(vectors * push_output_matrix, axis=4)
    return jnp.transpose(reduced_sum, (0, 3, 1, 2)).reshape(reduced_sum.shape[0], 3, -1)


def on_device(
    particle_places,
    particle_speeds,
    thermal_targets,
    element_features,
    swap_counterpart_slot,
    swap_approval_flags,
    initial_signal_projector,
    initial_distance_filter,
    initial_directional_scales,
    invariant_revision_matrix,
    magnitude_revision_matrix,
    later_signal_projector,
    later_directional_scales,
    push_output_matrix,
):
    replicas = particle_places.shape[0]
    local_cells = particle_places.shape[2] // NA
    channels = initial_signal_projector.shape[0]
    particle_number_overall = local_cells * lax.axis_size("dom") * NA
    near_species = with_halo(element_features, (("dom", 0),), HC * NA)
    first_table = jnp.dot(
        near_species, initial_signal_projector, preferred_element_type=jnp.float32
    ).astype(jnp.bfloat16)

    def evaluate(location_triples):
        near_coords = periodic_shift(with_halo(location_triples, (("dom", 2),), HC * NA), HC)
        hidden, vector_one = layer_one(
            near_coords,
            HC,
            local_cells,
            first_table,
            element_features,
            initial_distance_filter,
            initial_directional_scales,
            invariant_revision_matrix,
            magnitude_revision_matrix,
        )
        second_own = (
            jnp.dot(
                hidden.reshape(-1, channels),
                later_signal_projector,
                preferred_element_type=jnp.float32,
            )
            .astype(jnp.bfloat16)
            .reshape(replicas, -1, channels)
        )
        second_table = with_halo(second_own, (("dom", 1),), HC * NA)
        vector_two = layer_two(near_coords, HC, local_cells, second_table, later_directional_scales)
        return readout(vector_one + vector_two, push_output_matrix)

    location_triples = particle_places
    speed_entry = particle_speeds
    present_push = evaluate(location_triples)
    for step_index in range(STEPS):
        half_velocity = speed_entry + 0.5 * step_time * present_push
        location_triples = location_triples + step_time * half_velocity
        present_push = evaluate(location_triples)
        speed_entry = half_velocity + 0.5 * step_time * present_push
        motion_work_amount = lax.psum(jnp.sum(speed_entry * speed_entry, axis=(1, 2)), "dom")
        stretch_multiplier = jnp.sqrt(
            thermal_targets
            / (motion_work_amount / (3.0 * particle_number_overall) + motion_work_lower_limit)
        )
        speed_entry = speed_entry * stretch_multiplier[:, None, None]
    ladder_slot = jnp.arange(thermal_targets.shape[0], dtype=jnp.int32)
    source = jnp.where(swap_approval_flags > 0, swap_counterpart_slot, ladder_slot)
    selected_entries = (source[:, None] == ladder_slot[None, :]).astype(jnp.float32)

    def select_entries(values):
        return jnp.sum(selected_entries[:, :, None, None] * values[None], axis=1)

    thermal_ratio = jnp.sqrt(
        thermal_targets / jnp.sum(selected_entries * thermal_targets[None, :], axis=1)
    )
    atom_cell = (
        lax.axis_index("dom") * local_cells
        + jnp.arange(particle_places.shape[2], dtype=jnp.int32) // NA
    ).astype(jnp.float32)
    cell_floor = jnp.array([0.0, 0.0, 1.0], jnp.float32)[:, None] * atom_cell[None, :]
    return (
        select_entries(location_triples) - cell_floor[None],
        select_entries(speed_entry) * thermal_ratio[:, None, None],
        select_entries(present_push),
    )


def solution(mesh):
    return jax.shard_map(
        on_device,
        mesh=mesh,
        in_specs=(
            P("groups", None, "dom"),
            P("groups", None, "dom"),
            P("groups"),
            P(("groups", "dom"), None),
            P("groups"),
            P("groups"),
            P(),
            P(),
            P(),
            P(),
            P(),
            P(),
            P(),
            P(),
        ),
        out_specs=(P("groups", None, "dom"), P("groups", None, "dom"), P("groups", None, "dom")),
        check_vma=False,
    )
```

profile of v0, /device:TPU:0, one launch (start us, length us, event | category | flops | bytes accessed | tf_op | source)
XLA Modules:
  0.0 299.5 jit_solution(10295217078353361649)
XLA Ops:
  0.6 0.7 fusion.106
  1.4 0.5 collective-permute-start.2
  1.9 5.0 %collective-permute-start.3 = (f32[8,3,64]{2,0,1:T(8,128)S(1)}, f32[8,3,64]{2,0,1:T(8,128)S(1)}, u32[]{:S(2)}, u32[]{:S(2)}) collective-permute-start(f32[8,3,64]{2,0,1:T(8,128)S(1)} %get-tuple-element.66), channel_id=1, source_target_pairs={{1,0},{2,1},{3,2},{4,3},{5,4},{6,5},{7,6},{8,7},{9,8},{10,9},{11,1... | collective-permute-start | bytes 18440 | tf_op jit(solution)/shard_map/ppermute | solution.py:24
  6.9 0.7 fusion.96
  7.6 4.4 %collective-permute-start.1 = (bf16[64,128]{1,0:T(8,128)(2,1)S(1)}, bf16[64,128]{1,0:T(8,128)(2,1)S(1)}, u32[]{:S(2)}, u32[]{:S(2)}) collective-permute-start(bf16[64,128]{1,0:T(8,128)(2,1)S(1)} %get-tuple-element.41), channel_id=1, source_target_pairs={{1,0},{2,1},{3,2},{4,3},{5,4},{6,5},{7,6},{8,7},{9,8},{10,9},{11,1... | collective-permute-start | bytes 49160 | tf_op jit(solution)/shard_map/ppermute | solution.py:24
  12.0 0.7 broadcast_multiply_fusion.2
  12.8 0.8 convert_element_type.141
  13.6 0.8 maximum_add_fusion
  14.8 0.8 multiply_reduce_fusion.4
  15.7 5.1 %fusion.2 = bf16[8,3,64,8,192]{4,2,3,0,1:T(8,128)(2,1)} fusion(f32[8]{0:T(128)S(1)} %iota_multiply_fusion, f32[8,3,64,192]{3,2,1,0:T(8,128)S(1)} %multiply_reduce_fusion.4), kind=kLoop, calls=%fused_computation.7 | loop fusion | flops 12976128 | bytes 5898272 | tf_op jit(solution)/shard_map/convert.8
  20.9 1.2 multiply_convert_fusion.4
  22.3 5.0 %fusion.52 = f32[8,3,64,11,128]{4,2,3,0,1:T(8,128)S(1)} fusion(bf16[8,3,64,3,192]{4,2,3,0,1:T(8,128)(2,1)S(1)} %multiply_convert_fusion.4, bf16[8,3,64,8,192]{4,2,3,0,1:T(8,128)(2,1)} %fusion.2, bf16[3,64,128]{2,1,0:T(8,128)(2,1)S(1)} %bitcast.203, bf16[3,64,128]{2,1,0:T(8,128)(2,1)S(1)} %bitcast.208, bf16[3,64,128]{2,1,0:T(8,128)(2,1)S(1)} %bitcast.198), kind=kOutput, calls=%fused_computation.64 | convolution fusion | flops 843890688 | bytes 15286272 | tf_op jit(solution)/shard_map/vyegd,ydm->vyegm/dot_general | solution.py:106
  27.3 0.8 fusion.39
  29.7 4.4 %collective-permute-start.5 = (bf16[8,64,128]{2,1,0:T(8,128)(2,1)S(1)}, bf16[8,64,128]{2,1,0:T(8,128)(2,1)S(1)}, u32[]{:S(2)}, u32[]{:S(2)}) collective-permute-start(bf16[8,64,128]{2,1,0:T(8,128)(2,1)S(1)} %get-tuple-element.36), channel_id=1, source_target_pairs={{1,0},{2,1},{3,2},{4,3},{5,4},{6,5},{7,6},{8,7},{9,8},{10,9},{11,1... | collective-permute-start | bytes 393224 | tf_op jit(solution)/shard_map/ppermute | solution.py:24
  34.1 2.6 collective-permute-done.4
  36.9 2.0 multiply_reduce_fusion.13
  39.1 4.8 %collective-permute-start.7 = (f32[8,3,64]{2,0,1:T(8,128)S(1)}, f32[8,3,64]{2,0,1:T(8,128)S(1)}, u32[]{:S(2)}, u32[]{:S(2)}) collective-permute-start(f32[8,3,64]{2,0,1:T(8,128)S(1)} %get-tuple-element.64), channel_id=1, source_target_pairs={{1,0},{2,1},{3,2},{4,3},{5,4},{6,5},{7,6},{8,7},{9,8},{10,9},{11,1... | collective-permute-start | bytes 18440 | tf_op jit(solution)/shard_map/ppermute | solution.py:24
  43.9 1.1 collective-permute-done.6
  45.7 0.8 multiply_reduce_fusion.3
  46.6 5.1 %fusion.5 = bf16[8,3,64,8,192]{4,2,3,0,1:T(8,128)(2,1)} fusion(f32[8]{0:T(128)S(1)} %iota_multiply_fusion, f32[8,3,64,192]{3,2,1,0:T(8,128)S(1)} %multiply_reduce_fusion.3), kind=kLoop, calls=%fused_computation.10 | loop fusion | flops 12976128 | bytes 5898272 | tf_op jit(solution)/shard_map/convert.6
  51.8 1.2 multiply_convert_fusion.3
  53.0 5.0 %fusion.49 = f32[8,3,64,11,128]{4,2,3,0,1:T(8,128)S(1)} fusion(bf16[8,3,64,3,192]{4,2,3,0,1:T(8,128)(2,1)S(1)} %multiply_convert_fusion.3, bf16[8,3,64,8,192]{4,2,3,0,1:T(8,128)(2,1)} %fusion.5, bf16[3,64,128]{2,1,0:T(8,128)(2,1)S(1)} %bitcast.204, bf16[3,64,128]{2,1,0:T(8,128)(2,1)S(1)} %bitcast.209, bf16[3,64,128]{2,1,0:T(8,128)(2,1)S(1)} %bitcast.199), kind=kOutput, calls=%fused_computation.63 | convolution fusion | flops 843890688 | bytes 15286272 | tf_op jit(solution)/shard_map/vyegd,ydm->vyegm/dot_general | solution.py:106
  58.1 0.8 fusion.38
  60.2 4.5 %collective-permute-start.9 = (bf16[8,64,128]{2,1,0:T(8,128)(2,1)S(1)}, bf16[8,64,128]{2,1,0:T(8,128)(2,1)S(1)}, u32[]{:S(2)}, u32[]{:S(2)}) collective-permute-start(bf16[8,64,128]{2,1,0:T(8,128)(2,1)S(1)} %get-tuple-element.32), channel_id=1, source_target_pairs={{1,0},{2,1},{3,2},{4,3},{5,4},{6,5},{7,6},{8,7},{9,8},{10,9},{11,1... | collective-permute-start | bytes 393224 | tf_op jit(solution)/shard_map/ppermute | solution.py:24
  64.7 2.6 collective-permute-done.8
  67.4 2.0 multiply_reduce_fusion.11
  69.7 34.0 %psum.28 = f32[8]{0:T(128)S(1)} all-reduce(f32[8]{0:T(128)S(1)} %get-tuple-element.13), channel_id=1, replica_groups=mesh['groups'=2,'dom'=16] {'dom'}, use_global_device_ids=true, to_apply=%region_9.10 | all-reduce | flops 8 | bytes 64 | tf_op jit(solution)/shard_map/psum | solution.py:202
  103.8 4.4 %collective-permute-start.11 = (f32[8,3,64]{2,0,1:T(8,128)S(1)}, f32[8,3,64]{2,0,1:T(8,128)S(1)}, u32[]{:S(2)}, u32[]{:S(2)}) collective-permute-start(f32[8,3,64]{2,0,1:T(8,128)S(1)} %get-tuple-element.62), channel_id=1, source_target_pairs={{1,0},{2,1},{3,2},{4,3},{5,4},{6,5},{7,6},{8,7},{9,8},{10,9},{11,1... | collective-permute-start | bytes 18440 | tf_op jit(solution)/shard_map/ppermute | solution.py:24
  108.3 1.4 collective-permute-done.10
  110.1 0.8 multiply_reduce_fusion.2
  111.0 5.1 %fusion.8 = bf16[8,3,64,8,192]{4,2,3,0,1:T(8,128)(2,1)} fusion(f32[8]{0:T(128)S(1)} %iota_multiply_fusion, f32[8,3,64,192]{3,2,1,0:T(8,128)S(1)} %multiply_reduce_fusion.2), kind=kLoop, calls=%fused_computation.13 | loop fusion | flops 12976128 | bytes 5898272 | tf_op jit(solution)/shard_map/convert.4
  116.2 1.2 multiply_convert_fusion.2
  117.4 5.0 %fusion.46 = f32[8,3,64,11,128]{4,2,3,0,1:T(8,128)S(1)} fusion(bf16[8,3,64,3,192]{4,2,3,0,1:T(8,128)(2,1)S(1)} %multiply_convert_fusion.2, bf16[8,3,64,8,192]{4,2,3,0,1:T(8,128)(2,1)} %fusion.8, bf16[3,64,128]{2,1,0:T(8,128)(2,1)S(1)} %bitcast.205, bf16[3,64,128]{2,1,0:T(8,128)(2,1)S(1)} %bitcast.210, bf16[3,64,128]{2,1,0:T(8,128)(2,1)S(1)} %bitcast.200), kind=kOutput, calls=%fused_computation.62 | convolution fusion | flops 843890688 | bytes 15286272 | tf_op jit(solution)/shard_map/vyegd,ydm->vyegm/dot_general | solution.py:106
  122.4 0.8 fusion.37
  123.8 0.4 fusion.62
  124.5 4.5 %collective-permute-start.13 = (bf16[8,64,128]{2,1,0:T(8,128)(2,1)S(1)}, bf16[8,64,128]{2,1,0:T(8,128)(2,1)S(1)}, u32[]{:S(2)}, u32[]{:S(2)}) collective-permute-start(bf16[8,64,128]{2,1,0:T(8,128)(2,1)S(1)} %get-tuple-element.28), channel_id=1, source_target_pairs={{1,0},{2,1},{3,2},{4,3},{5,4},{6,5},{7,6},{8,7},{9,8},{10,9},{11,1... | collective-permute-start | bytes 393224 | tf_op jit(solution)/shard_map/ppermute | solution.py:24
  129.0 2.6 collective-permute-done.12
  131.7 2.0 multiply_reduce_fusion.9
  134.1 34.0 %psum.29 = f32[8]{0:T(128)S(1)} all-reduce(f32[8]{0:T(128)S(1)} %get-tuple-element.11), channel_id=1, replica_groups=mesh['groups'=2,'dom'=16] {'dom'}, use_global_device_ids=true, to_apply=%region_15.16 | all-reduce | flops 8 | bytes 64 | tf_op jit(solution)/shard_map/psum | solution.py:202
  168.2 4.4 %collective-permute-start.15 = (f32[8,3,64]{2,0,1:T(8,128)S(1)}, f32[8,3,64]{2,0,1:T(8,128)S(1)}, u32[]{:S(2)}, u32[]{:S(2)}) collective-permute-start(f32[8,3,64]{2,0,1:T(8,128)S(1)} %get-tuple-element.60), channel_id=1, source_target_pairs={{1,0},{2,1},{3,2},{4,3},{5,4},{6,5},{7,6},{8,7},{9,8},{10,9},{11,1... | collective-permute-start | bytes 18440 | tf_op jit(solution)/shard_map/ppermute | solution.py:24
  172.6 1.4 collective-permute-done.14
  174.4 0.8 multiply_reduce_fusion.1
  175.3 5.1 %fusion.11 = bf16[8,3,64,8,192]{4,2,3,0,1:T(8,128)(2,1)} fusion(f32[8]{0:T(128)S(1)} %iota_multiply_fusion, f32[8,3,64,192]{3,2,1,0:T(8,128)S(1)} %multiply_reduce_fusion.1), kind=kLoop, calls=%fused_computation.16 | loop fusion | flops 12976128 | bytes 5898272 | tf_op jit(solution)/shard_map/convert.2
  180.5 1.2 multiply_convert_fusion.1
  181.7 5.0 %fusion.43 = f32[8,3,64,11,128]{4,2,3,0,1:T(8,128)S(1)} fusion(bf16[8,3,64,3,192]{4,2,3,0,1:T(8,128)(2,1)S(1)} %multiply_convert_fusion.1, bf16[8,3,64,8,192]{4,2,3,0,1:T(8,128)(2,1)} %fusion.11, bf16[3,64,128]{2,1,0:T(8,128)(2,1)S(1)} %bitcast.206, bf16[3,64,128]{2,1,0:T(8,128)(2,1)S(1)} %bitcast.211, bf16[3,64,128]{2,1,0:T(8,128)(2,1)S(1)} %bitcast.201), kind=kOutput, calls=%fused_computation.61 | convolution fusion | flops 843890688 | bytes 15286272 | tf_op jit(solution)/shard_map/vyegd,ydm->vyegm/dot_general | solution.py:106
  186.8 0.8 fusion.36
  189.2 4.5 %collective-permute-start.17 = (bf16[8,64,128]{2,1,0:T(8,128)(2,1)S(1)}, bf16[8,64,128]{2,1,0:T(8,128)(2,1)S(1)}, u32[]{:S(2)}, u32[]{:S(2)}) collective-permute-start(bf16[8,64,128]{2,1,0:T(8,128)(2,1)S(1)} %get-tuple-element.24), channel_id=1, source_target_pairs={{1,0},{2,1},{3,2},{4,3},{5,4},{6,5},{7,6},{8,7},{9,8},{10,9},{11,1... | collective-permute-start | bytes 393224 | tf_op jit(solution)/shard_map/ppermute | solution.py:24
  193.6 2.6 collective-permute-done.16
  196.4 2.0 multiply_reduce_fusion.7
  198.8 33.9 %psum.30 = f32[8]{0:T(128)S(1)} all-reduce(f32[8]{0:T(128)S(1)} %multiply_reduce_fusion.19), channel_id=1, replica_groups=mesh['groups'=2,'dom'=16] {'dom'}, use_global_device_ids=true, to_apply=%region_21.22 | all-reduce | flops 8 | bytes 64 | tf_op jit(solution)/shard_map/psum | solution.py:202
  232.9 4.4 %collective-permute-start.19 = (f32[8,3,64]{2,0,1:T(8,128)S(1)}, f32[8,3,64]{2,0,1:T(8,128)S(1)}, u32[]{:S(2)}, u32[]{:S(2)}) collective-permute-start(f32[8,3,64]{2,0,1:T(8,128)S(1)} %get-tuple-element.58), channel_id=1, source_target_pairs={{1,0},{2,1},{3,2},{4,3},{5,4},{6,5},{7,6},{8,7},{9,8},{10,9},{11,1... | collective-permute-start | bytes 18440 | tf_op jit(solution)/shard_map/ppermute | solution.py:24
  237.4 1.4 collective-permute-done.18
  239.2 0.8 multiply_reduce_fusion
  240.1 5.1 %fusion.14 = bf16[8,3,64,8,192]{4,2,3,0,1:T(8,128)(2,1)} fusion(f32[8]{0:T(128)S(1)} %iota_multiply_fusion, f32[8,3,64,192]{3,2,1,0:T(8,128)S(1)} %multiply_reduce_fusion), kind=kLoop, calls=%fused_computation.19 | loop fusion | flops 12976128 | bytes 5898272 | tf_op jit(solution)/shard_map/convert
  245.3 1.2 multiply_convert_fusion
  246.5 5.0 %fusion.40 = f32[8,3,64,11,128]{4,2,3,0,1:T(8,128)S(1)} fusion(bf16[8,3,64,3,192]{4,2,3,0,1:T(8,128)(2,1)S(1)} %multiply_convert_fusion, bf16[8,3,64,8,192]{4,2,3,0,1:T(8,128)(2,1)} %fusion.14, bf16[3,64,128]{2,1,0:T(8,128)(2,1)S(1)} %bitcast.207, bf16[3,64,128]{2,1,0:T(8,128)(2,1)S(1)} %bitcast.212, bf16[3,64,128]{2,1,0:T(8,128)(2,1)S(1)} %bitcast.202), kind=kOutput, calls=%fused_computation.60 | convolution fusion | flops 843890688 | bytes 15286272 | tf_op jit(solution)/shard_map/vyegd,ydm->vyegm/dot_general | solution.py:106
  251.5 0.8 fusion.35
  253.6 4.5 %collective-permute-start.21 = (bf16[8,64,128]{2,1,0:T(8,128)(2,1)S(1)}, bf16[8,64,128]{2,1,0:T(8,128)(2,1)S(1)}, u32[]{:S(2)}, u32[]{:S(2)}) collective-permute-start(bf16[8,64,128]{2,1,0:T(8,128)(2,1)S(1)} %get-tuple-element.20), channel_id=1, source_target_pairs={{1,0},{2,1},{3,2},{4,3},{5,4},{6,5},{7,6},{8,7},{9,8},{10,9},{11,1... | collective-permute-start | bytes 393224 | tf_op jit(solution)/shard_map/ppermute | solution.py:24
  258.2 2.5 collective-permute-done.20
  260.8 2.0 multiply_reduce_fusion.5
  263.3 34.0 %psum.31 = f32[8]{0:T(128)S(1)} all-reduce(f32[8]{0:T(128)S(1)} %multiply_reduce_fusion.18), channel_id=1, replica_groups=mesh['groups'=2,'dom'=16] {'dom'}, use_global_device_ids=true, to_apply=%region_28.29 | all-reduce | flops 8 | bytes 64 | tf_op jit(solution)/shard_map/psum | solution.py:202
  297.6 0.6 copy.245
  298.3 0.6 copy.246
  298.9 0.6 copy.247
  (173 shorter events, 13.1 us)
Async XLA Ops:
  0.6 27.9 %copy-start = (bf16[128,128]{1,0:T(8,128)(2,1)S(1)}, bf16[128,128]{1,0:T(8,128)(2,1)}, u32[]{:S(2)}) copy-start(bf16[128,128]{1,0:T(8,128)(2,1)} %param.29) | copy-start | bytes 98308
  1.4 12.2 %collective-permute-start.2 = (f32[8,3,64]{2,0,1:T(8,128)S(1)}, f32[8,3,64]{2,0,1:T(8,128)S(1)}, u32[]{:S(2)}, u32[]{:S(2)}) collective-permute-start(f32[8,3,64]{2,0,1:T(8,128)S(1)} %get-tuple-element.65), channel_id=1, source_target_pairs={{0,1},{1,2},{2,3},{3,4},{4,5},{5,6},{6,7},{7,8},{8,9},{9,10},{10,1... | collective-permute-start | bytes 18440 | tf_op jit(solution)/shard_map/ppermute | solution.py:22
  1.9 11.7 %collective-permute-start.3 = (f32[8,3,64]{2,0,1:T(8,128)S(1)}, f32[8,3,64]{2,0,1:T(8,128)S(1)}, u32[]{:S(2)}, u32[]{:S(2)}) collective-permute-start(f32[8,3,64]{2,0,1:T(8,128)S(1)} %get-tuple-element.66), channel_id=1, source_target_pairs={{1,0},{2,1},{3,2},{4,3},{5,4},{6,5},{7,6},{8,7},{9,8},{10,9},{11,1... | collective-permute-start | bytes 18440 | tf_op jit(solution)/shard_map/ppermute | solution.py:24
  7.6 14.4 %collective-permute-start = (bf16[64,128]{1,0:T(8,128)(2,1)S(1)}, bf16[64,128]{1,0:T(8,128)(2,1)S(1)}, u32[]{:S(2)}, u32[]{:S(2)}) collective-permute-start(bf16[64,128]{1,0:T(8,128)(2,1)S(1)} %get-tuple-element.40), channel_id=1, source_target_pairs={{0,1},{1,2},{2,3},{3,4},{4,5},{5,6},{6,7},{7,8},{8,9},{9,10},{10,1... | collective-permute-start | bytes 49160 | tf_op jit(solution)/shard_map/ppermute | solution.py:22
  7.6 14.4 %collective-permute-start.1 = (bf16[64,128]{1,0:T(8,128)(2,1)S(1)}, bf16[64,128]{1,0:T(8,128)(2,1)S(1)}, u32[]{:S(2)}, u32[]{:S(2)}) collective-permute-start(bf16[64,128]{1,0:T(8,128)(2,1)S(1)} %get-tuple-element.41), channel_id=1, source_target_pairs={{1,0},{2,1},{3,2},{4,3},{5,4},{6,5},{7,6},{8,7},{9,8},{10,9},{11,1... | collective-permute-start | bytes 49160 | tf_op jit(solution)/shard_map/ppermute | solution.py:24
  20.8 1.2 copy-start.4
  20.8 1.2 copy-start.10
  22.3 5.1 %copy-start.5 = (f32[8,128]{1,0:T(8,128)S(1)}, f32[8,128]{1,0:T(8,128)}, u32[]{:S(2)}) copy-start(f32[8,128]{1,0:T(8,128)} %param.27) | copy-start | bytes 12292
  27.3 0.8 copy-start.7
  28.2 0.8 copy-start.2
  28.5 0.9 copy-start.1
  28.8 8.1 %copy-start.13 = (f32[128]{0:T(128)S(1)}, f32[128]{0:T(128)}, u32[]{:S(2)}) copy-start(f32[128]{0:T(128)} %param.33) | copy-start | bytes 1540
  28.8 8.1 %copy-start.14 = (f32[128]{0:T(128)S(1)}, f32[128]{0:T(128)}, u32[]{:S(2)}) copy-start(f32[128]{0:T(128)} %param.32) | copy-start | bytes 1540
  29.6 7.1 %collective-permute-start.4 = (bf16[8,64,128]{2,1,0:T(8,128)(2,1)S(1)}, bf16[8,64,128]{2,1,0:T(8,128)(2,1)S(1)}, u32[]{:S(2)}, u32[]{:S(2)}) collective-permute-start(bf16[8,64,128]{2,1,0:T(8,128)(2,1)S(1)} %get-tuple-element.35), channel_id=1, source_target_pairs={{0,1},{1,2},{2,3},{3,4},{4,5},{5,6},{6,7},{7,8},{8,9},{9,10},{10,1... | collective-permute-start | bytes 393224 | tf_op jit(solution)/shard_map/ppermute | solution.py:22
  29.7 7.1 %collective-permute-start.5 = (bf16[8,64,128]{2,1,0:T(8,128)(2,1)S(1)}, bf16[8,64,128]{2,1,0:T(8,128)(2,1)S(1)}, u32[]{:S(2)}, u32[]{:S(2)}) collective-permute-start(bf16[8,64,128]{2,1,0:T(8,128)(2,1)S(1)} %get-tuple-element.36), channel_id=1, source_target_pairs={{1,0},{2,1},{3,2},{4,3},{5,4},{6,5},{7,6},{8,7},{9,8},{10,9},{11,1... | collective-permute-start | bytes 393224 | tf_op jit(solution)/shard_map/ppermute | solution.py:24
  36.9 2.2 copy-start.3
  36.9 2.2 copy-start.6
  39.1 6.0 %collective-permute-start.6 = (f32[8,3,64]{2,0,1:T(8,128)S(1)}, f32[8,3,64]{2,0,1:T(8,128)S(1)}, u32[]{:S(2)}, u32[]{:S(2)}) collective-permute-start(f32[8,3,64]{2,0,1:T(8,128)S(1)} %get-tuple-element.63), channel_id=1, source_target_pairs={{0,1},{1,2},{2,3},{3,4},{4,5},{5,6},{6,7},{7,8},{8,9},{9,10},{10,1... | collective-permute-start | bytes 18440 | tf_op jit(solution)/shard_map/ppermute | solution.py:22
  39.1 6.2 %collective-permute-start.7 = (f32[8,3,64]{2,0,1:T(8,128)S(1)}, f32[8,3,64]{2,0,1:T(8,128)S(1)}, u32[]{:S(2)}, u32[]{:S(2)}) collective-permute-start(f32[8,3,64]{2,0,1:T(8,128)S(1)} %get-tuple-element.64), channel_id=1, source_target_pairs={{1,0},{2,1},{3,2},{4,3},{5,4},{6,5},{7,6},{8,7},{9,8},{10,9},{11,1... | collective-permute-start | bytes 18440 | tf_op jit(solution)/shard_map/ppermute | solution.py:24
  60.1 7.1 %collective-permute-start.8 = (bf16[8,64,128]{2,1,0:T(8,128)(2,1)S(1)}, bf16[8,64,128]{2,1,0:T(8,128)(2,1)S(1)}, u32[]{:S(2)}, u32[]{:S(2)}) collective-permute-start(bf16[8,64,128]{2,1,0:T(8,128)(2,1)S(1)} %get-tuple-element.31), channel_id=1, source_target_pairs={{0,1},{1,2},{2,3},{3,4},{4,5},{5,6},{6,7},{7,8},{8,9},{9,10},{10,1... | collective-permute-start | bytes 393224 | tf_op jit(solution)/shard_map/ppermute | solution.py:22
  60.2 7.1 %collective-permute-start.9 = (bf16[8,64,128]{2,1,0:T(8,128)(2,1)S(1)}, bf16[8,64,128]{2,1,0:T(8,128)(2,1)S(1)}, u32[]{:S(2)}, u32[]{:S(2)}) collective-permute-start(bf16[8,64,128]{2,1,0:T(8,128)(2,1)S(1)} %get-tuple-element.32), channel_id=1, source_target_pairs={{1,0},{2,1},{3,2},{4,3},{5,4},{6,5},{7,6},{8,7},{9,8},{10,9},{11,1... | collective-permute-start | bytes 393224 | tf_op jit(solution)/shard_map/ppermute | solution.py:24
  67.4 36.3 %copy-start.9 = (f32[8]{0:T(128)S(1)}, f32[8]{0:T(128)}, u32[]{:S(2)}) copy-start(f32[8]{0:T(128)} %param.22) | copy-start | bytes 100
  103.8 5.9 %collective-permute-start.10 = (f32[8,3,64]{2,0,1:T(8,128)S(1)}, f32[8,3,64]{2,0,1:T(8,128)S(1)}, u32[]{:S(2)}, u32[]{:S(2)}) collective-permute-start(f32[8,3,64]{2,0,1:T(8,128)S(1)} %get-tuple-element.61), channel_id=1, source_target_pairs={{0,1},{1,2},{2,3},{3,4},{4,5},{5,6},{6,7},{7,8},{8,9},{9,10},{10,1... | collective-permute-start | bytes 18440 | tf_op jit(solution)/shard_map/ppermute | solution.py:22
  103.8 5.8 %collective-permute-start.11 = (f32[8,3,64]{2,0,1:T(8,128)S(1)}, f32[8,3,64]{2,0,1:T(8,128)S(1)}, u32[]{:S(2)}, u32[]{:S(2)}) collective-permute-start(f32[8,3,64]{2,0,1:T(8,128)S(1)} %get-tuple-element.62), channel_id=1, source_target_pairs={{1,0},{2,1},{3,2},{4,3},{5,4},{6,5},{7,6},{8,7},{9,8},{10,9},{11,1... | collective-permute-start | bytes 18440 | tf_op jit(solution)/shard_map/ppermute | solution.py:24
  124.5 7.1 %collective-permute-start.12 = (bf16[8,64,128]{2,1,0:T(8,128)(2,1)S(1)}, bf16[8,64,128]{2,1,0:T(8,128)(2,1)S(1)}, u32[]{:S(2)}, u32[]{:S(2)}) collective-permute-start(bf16[8,64,128]{2,1,0:T(8,128)(2,1)S(1)} %get-tuple-element.27), channel_id=1, source_target_pairs={{0,1},{1,2},{2,3},{3,4},{4,5},{5,6},{6,7},{7,8},{8,9},{9,10},{10,1... | collective-permute-start | bytes 393224 | tf_op jit(solution)/shard_map/ppermute | solution.py:22
  124.5 7.1 %collective-permute-start.13 = (bf16[8,64,128]{2,1,0:T(8,128)(2,1)S(1)}, bf16[8,64,128]{2,1,0:T(8,128)(2,1)S(1)}, u32[]{:S(2)}, u32[]{:S(2)}) collective-permute-start(bf16[8,64,128]{2,1,0:T(8,128)(2,1)S(1)} %get-tuple-element.28), channel_id=1, source_target_pairs={{1,0},{2,1},{3,2},{4,3},{5,4},{6,5},{7,6},{8,7},{9,8},{10,9},{11,1... | collective-permute-start | bytes 393224 | tf_op jit(solution)/shard_map/ppermute | solution.py:24
  168.1 5.9 %collective-permute-start.14 = (f32[8,3,64]{2,0,1:T(8,128)S(1)}, f32[8,3,64]{2,0,1:T(8,128)S(1)}, u32[]{:S(2)}, u32[]{:S(2)}) collective-permute-start(f32[8,3,64]{2,0,1:T(8,128)S(1)} %get-tuple-element.59), channel_id=1, source_target_pairs={{0,1},{1,2},{2,3},{3,4},{4,5},{5,6},{6,7},{7,8},{8,9},{9,10},{10,1... | collective-permute-start | bytes 18440 | tf_op jit(solution)/shard_map/ppermute | solution.py:22
  168.2 5.8 %collective-permute-start.15 = (f32[8,3,64]{2,0,1:T(8,128)S(1)}, f32[8,3,64]{2,0,1:T(8,128)S(1)}, u32[]{:S(2)}, u32[]{:S(2)}) collective-permute-start(f32[8,3,64]{2,0,1:T(8,128)S(1)} %get-tuple-element.60), channel_id=1, source_target_pairs={{1,0},{2,1},{3,2},{4,3},{5,4},{6,5},{7,6},{8,7},{9,8},{10,9},{11,1... | collective-permute-start | bytes 18440 | tf_op jit(solution)/shard_map/ppermute | solution.py:24
  188.8 7.4 %collective-permute-start.16 = (bf16[8,64,128]{2,1,0:T(8,128)(2,1)S(1)}, bf16[8,64,128]{2,1,0:T(8,128)(2,1)S(1)}, u32[]{:S(2)}, u32[]{:S(2)}) collective-permute-start(bf16[8,64,128]{2,1,0:T(8,128)(2,1)S(1)} %get-tuple-element.23), channel_id=1, source_target_pairs={{0,1},{1,2},{2,3},{3,4},{4,5},{5,6},{6,7},{7,8},{8,9},{9,10},{10,1... | collective-permute-start | bytes 393224 | tf_op jit(solution)/shard_map/ppermute | solution.py:22
  189.2 7.1 %collective-permute-start.17 = (bf16[8,64,128]{2,1,0:T(8,128)(2,1)S(1)}, bf16[8,64,128]{2,1,0:T(8,128)(2,1)S(1)}, u32[]{:S(2)}, u32[]{:S(2)}) collective-permute-start(bf16[8,64,128]{2,1,0:T(8,128)(2,1)S(1)} %get-tuple-element.24), channel_id=1, source_target_pairs={{1,0},{2,1},{3,2},{4,3},{5,4},{6,5},{7,6},{8,7},{9,8},{10,9},{11,1... | collective-permute-start | bytes 393224 | tf_op jit(solution)/shard_map/ppermute | solution.py:24
  196.3 2.4 copy-start.8
  196.4 41.0 %copy-start.11 = (s32[8]{0:T(128)S(1)}, s32[8]{0:T(128)}, u32[]{:S(2)}) copy-start(s32[8]{0:T(128)} %param.24) | copy-start | bytes 100
  196.4 41.0 %copy-start.12 = (s32[8]{0:T(128)S(1)}, s32[8]{0:T(128)}, u32[]{:S(2)}) copy-start(s32[8]{0:T(128)} %param.25) | copy-start | bytes 100
  232.9 5.9 %collective-permute-start.18 = (f32[8,3,64]{2,0,1:T(8,128)S(1)}, f32[8,3,64]{2,0,1:T(8,128)S(1)}, u32[]{:S(2)}, u32[]{:S(2)}) collective-permute-start(f32[8,3,64]{2,0,1:T(8,128)S(1)} %get-tuple-element.57), channel_id=1, source_target_pairs={{0,1},{1,2},{2,3},{3,4},{4,5},{5,6},{6,7},{7,8},{8,9},{9,10},{10,1... | collective-permute-start | bytes 18440 | tf_op jit(solution)/shard_map/ppermute | solution.py:22
  232.9 5.8 %collective-permute-start.19 = (f32[8,3,64]{2,0,1:T(8,128)S(1)}, f32[8,3,64]{2,0,1:T(8,128)S(1)}, u32[]{:S(2)}, u32[]{:S(2)}) collective-permute-start(f32[8,3,64]{2,0,1:T(8,128)S(1)} %get-tuple-element.58), channel_id=1, source_target_pairs={{1,0},{2,1},{3,2},{4,3},{5,4},{6,5},{7,6},{8,7},{9,8},{10,9},{11,1... | collective-permute-start | bytes 18440 | tf_op jit(solution)/shard_map/ppermute | solution.py:24
  253.6 7.1 %collective-permute-start.20 = (bf16[8,64,128]{2,1,0:T(8,128)(2,1)S(1)}, bf16[8,64,128]{2,1,0:T(8,128)(2,1)S(1)}, u32[]{:S(2)}, u32[]{:S(2)}) collective-permute-start(bf16[8,64,128]{2,1,0:T(8,128)(2,1)S(1)} %get-tuple-element.19), channel_id=1, source_target_pairs={{0,1},{1,2},{2,3},{3,4},{4,5},{5,6},{6,7},{7,8},{8,9},{9,10},{10,1... | collective-permute-start | bytes 393224 | tf_op jit(solution)/shard_map/ppermute | solution.py:22
  253.6 7.1 %collective-permute-start.21 = (bf16[8,64,128]{2,1,0:T(8,128)(2,1)S(1)}, bf16[8,64,128]{2,1,0:T(8,128)(2,1)S(1)}, u32[]{:S(2)}, u32[]{:S(2)}) collective-permute-start(bf16[8,64,128]{2,1,0:T(8,128)(2,1)S(1)} %get-tuple-element.20), channel_id=1, source_target_pairs={{1,0},{2,1},{3,2},{4,3},{5,4},{6,5},{7,6},{8,7},{9,8},{10,9},{11,1... | collective-permute-start | bytes 393224 | tf_op jit(solution)/shard_map/ppermute | solution.py:24
where the time goes:
time: 300 us; the launch traced here: 299 us
  blocking collectives  136 us (45%)
  starting transfers between devices  51 us (17%)
  other arithmetic  46 us (15%)
  matrix products  39.7 us (13%)
  waiting for transfers between devices  18.7 us (6%)
  local copies, waits for them, and re-layouts  6.62 us (2%)
    psum x4, blocking collectives, on_device(): lax.psum(jnp.sum(speed_entry * speed_entry, axis=(1, 2)), 'dom')  136 us
    ppermute x11, starting transfers between devices, with_halo(): lax.ppermute(head, axis, [((i + 1) % count, i) for i in range(count)])  49.8 us
    another operation x10, other arithmetic  31.5 us
    dot_general x5, matrix products, layer_one(): jnp.einsum('vyegd,ydm->vyegm', single_row_count, exchange_mate, preferred...  25.2 us
    ppermute x11, waiting for transfers between devices, with_halo(): lax.ppermute(tail, axis, [(i, (i + 1) % count) for i in range(count)])  18.3 us
    dot_general x5, matrix products, layer_two(): jnp.einsum('rcaxb,rcbf->rcaxf', rows_two, exchange_mate, preferred_elemen...  9.99 us
  transfers between devices with their start and end apart: 22, of which 10 were waited for; matrix products, arithmetic and copies ran while one was open for 4% of the time, Pallas kernels for 0%

commit v1 on v0

v1 whole, which is shorter than its diff:
```python
import functools
import math

import jax
import jax.numpy as jnp
from jax import lax
from jax.experimental import pallas as pl
from jax.experimental.pallas import tpu as pltpu
from jax.sharding import PartitionSpec as P

NA = 64
STEPS = 4
LANES = 128
CHUNK = 32

step_time = 0.05
motion_work_lower_limit = 1e-06

F32 = jnp.float32
BF16 = jnp.bfloat16
MESH = pl.DeviceIdType.MESH
NT = (((1,), (1,)), ((), ()))


def split_bf16(values):
    high = values.astype(BF16)
    low = (values - high.astype(F32)).astype(BF16)
    return high, low


def weight_rows(weights):
    high, low = split_bf16(weights)
    high, low = high.astype(F32), low.astype(F32)
    row = lax.broadcasted_iota(jnp.int32, (16, weights.shape[1]), 0)
    return jnp.where(row == 0, high, jnp.where(row == 1, low, 0.0)).astype(BF16)


def pair_base(rows, columns):
    dx, dy, dz = [row - column for row, column in zip(rows, columns)]
    squared = dx * dx + dy * dy + dz * dz
    inside = jnp.maximum(1.0 - squared, 0.0)
    envelope = inside * inside
    centered = jnp.minimum(squared, 1.0) - 0.5
    return (dx * envelope, dy * envelope, dz * envelope), envelope, centered


def kernel(
    n, replicas, cells, group,
    places, speeds, targets, slots, flags, features,
    projector, radial_filter, scales_one, invariant, magnitude, later_projector, scales_two, push,
    places_out, speeds_out, forces_out,
    feature_halo, place_send, place_halo, table_one, table_vec, s_one,
    state_x, state_v, state_g, win, columns, gauss, vectors, s_own,
    s_send, s_recv, vg_send, vg_recv, kin_send, kin_recv,
    init_send_sem, init_recv_sem, s_send_sem, s_recv_sem, vg_send_sem, vg_recv_sem,
    kin_send_sem, kin_recv_sem,
):
    me = lax.axis_index("dom")
    left = lax.rem(me + n - 1, n)
    right = lax.rem(me + 1, n)
    own = cells * NA
    width = state_x.shape[2]
    right_at, left_at = own, own + NA
    channels = features.shape[1]

    def cell_at(c):
        return left_at if c < 0 else c * NA

    barrier = pltpu.get_barrier_semaphore()

    def greet(d, carry):
        pl.semaphore_signal(barrier, inc=1, device_id={"dom": lax.rem(me + d, n)}, device_id_type=MESH)
        return carry

    lax.fori_loop(1, n, greet, 0)

    zeros_pad = jnp.zeros((replicas, width - own), F32)
    for c in range(3):
        x = places[:, c, :]
        place_send[c] = jnp.concatenate([x[:, :NA], x[:, own - NA:]], axis=1)
        state_x[c, :, :] = jnp.concatenate([x, zeros_pad], axis=1)
        state_v[c, :, :] = jnp.concatenate([speeds[:, c, :], zeros_pad], axis=1)
        state_g[c, :, :] = jnp.zeros((replicas, width), F32)

    pl.semaphore_wait(barrier, n - 1)

    def remote(src, dst, send_sem, recv_sem, to):
        return pltpu.make_async_remote_copy(
            src_ref=src, dst_ref=dst, send_sem=send_sem, recv_sem=recv_sem,
            device_id={"dom": to}, device_id_type=MESH,
        )

    first = [
        remote(place_send, place_halo.at[1], init_send_sem.at[0], init_recv_sem.at[0], left),
        remote(place_send, place_halo.at[0], init_send_sem.at[1], init_recv_sem.at[1], right),
        remote(features.at[pl.ds(0, NA)], feature_halo.at[1], init_send_sem.at[2], init_recv_sem.at[2], left),
        remote(features.at[pl.ds(own - NA, NA)], feature_halo.at[0], init_send_sem.at[3], init_recv_sem.at[3], right),
    ]
    for copy in first:
        copy.start()

    filters = radial_filter[...]
    push_row = push[...]
    w_one = weight_rows(scales_one[...] * push_row)
    w_two = weight_rows(scales_two[...] * push_row)
    scale_row = scales_one[...]

    def make_table(rows):
        return jnp.dot(rows, projector[...], preferred_element_type=F32).astype(BF16)

    tables = {c: make_table(features[c * NA:(c + 1) * NA, :]) for c in range(cells)}
    for copy in first:
        copy.wait()
    tables[-1] = make_table(feature_halo[0])
    tables[cells] = make_table(feature_halo[1])

    s_parts = []
    for c in list(range(cells)) + [cells, -1]:
        out = lax.dot_general(w_one, tables[c], NT, preferred_element_type=F32)
        s_parts.append(out[0:1] + out[1:2])
    s_one[...] = jnp.concatenate(s_parts + [jnp.zeros((1, width - own - 2 * NA), F32)], axis=1)

    for c in range(cells):
        before, here, after = [tables[c + j].astype(F32) for j in (-1, 0, 1)]
        table_vec[c, 0:NA, :] = tables[c - 1]
        table_vec[c, NA:2 * NA, :] = tables[c]
        table_vec[c, 2 * NA:3 * NA, :] = tables[c + 1]
        table_vec[c, 3 * NA:4 * NA, :] = jnp.zeros((NA, channels), BF16)
        for k in range(8):
            row = filters[k:k + 1]
            table_one[c, k * LANES:k * LANES + NA, :] = (before * row).astype(BF16)
            table_one[c, k * LANES + NA:(k + 1) * LANES, :] = (here * row).astype(BF16)
        for j in range(4):
            at = (8 + j) * LANES
            table_one[c, at:at + NA, :] = (after * filters[4 + j:5 + j]).astype(BF16)
            table_one[c, at + NA:at + LANES, :] = (after * filters[3 - j:4 - j]).astype(BF16)

    for c in range(3):
        state_x[c, :, right_at:right_at + NA] = place_halo[1, c, :, 0:NA]
        state_x[c, :, left_at:left_at + NA] = place_halo[0, c, :, NA:2 * NA]

    total = float(cells * n)
    lane = lax.broadcasted_iota(jnp.int32, (1, width), 1)
    up = jnp.where(me == n - 1, total, 0.0).astype(F32)
    down = jnp.where(me == 0, -total, 0.0).astype(F32)
    shift = jnp.where(
        (lane >= right_at) & (lane < right_at + NA), up,
        jnp.where((lane >= left_at) & (lane < left_at + NA), down, 0.0),
    )
    side = jnp.where(lax.broadcasted_iota(jnp.int32, (1, LANES), 1) < NA, 14.0, -14.0).astype(F32)
    replica_row = lax.broadcasted_iota(jnp.int32, (replicas, 1), 0)
    diagonal = (
        lax.broadcasted_iota(jnp.int32, (replicas, LANES), 0)
        == lax.broadcasted_iota(jnp.int32, (replicas, LANES), 1)
    )
    target = jnp.zeros((replicas, 1), F32)
    source = jnp.zeros((replicas, 1), jnp.int32)
    for r in range(replicas):
        target = jnp.where(replica_row == r, targets[r], target)
        source = jnp.where(replica_row == r, jnp.where(flags[r] > 0, slots[r], r), source)

    ratio = math.exp(-4.0)

    def chain(start, power):
        values = [start]
        for _ in range(3):
            values.append(values[-1] * power)
            power = power * ratio
        return values

    def build(c, r, slot):
        rows = [win[c, d, r:r + 1, :] for d in range(3)]
        for at in range(0, NA, CHUNK):
            here = slice(at, at + CHUNK)
            cols = [
                columns[c * NA + at:c * NA + at + CHUNK, d * replicas + r:d * replicas + r + 1]
                for d in range(3)
            ]
            cols = [jnp.broadcast_to(col, (CHUNK, LANES)) for col in cols]
            vec, envelope, t = pair_base([row[:, :LANES] for row in rows], cols)
            for d in range(3):
                vectors[c, r, d * NA + at:d * NA + at + CHUNK, 0:LANES] = vec[d].astype(BF16)
            base = jnp.exp(-98.0 * (t * t) - 0.5) * envelope
            grow = jnp.exp(14.0 * t)
            shrink = jnp.exp(-14.0 * t)
            high = chain(base * grow, grow * grow * ratio)
            low = chain(base * shrink, shrink * shrink * ratio)
            out = slice(slot * NA + at, slot * NA + at + CHUNK)
            for j in range(4):
                gauss[out, (4 + j) * LANES:(5 + j) * LANES] = high[j].astype(BF16)
                gauss[out, (3 - j) * LANES:(4 - j) * LANES] = low[j].astype(BF16)
            vec, envelope, t = pair_base([row[:, LANES:] for row in rows], cols)
            for d in range(3):
                vectors[c, r, d * NA + at:d * NA + at + CHUNK, LANES:] = vec[d].astype(BF16)
            base = jnp.exp(-98.0 * (t * t) - 0.5) * envelope
            grow = jnp.exp(side * t)
            both = chain(base * grow, grow * grow * ratio)
            for j in range(4):
                gauss[out, (8 + j) * LANES:(9 + j) * LANES] = both[j].astype(BF16)

    def layer_one(c, part):
        members = range(part * group, (part + 1) * group)
        base = part * group * NA
        for r in members:
            build(c, r, r)
        scalar = jnp.dot(
            gauss[base:base + group * NA, :], table_one[c], preferred_element_type=F32
        ).astype(BF16)
        norms = []
        for r in members:
            vec = jnp.dot(vectors[c, r], table_vec[c], preferred_element_type=F32)
            square = 0.0
            for d in range(3):
                one = vec[d * NA:(d + 1) * NA] * scale_row
                square = square + one * one
            norms.append(square.astype(BF16))
        norm = jnp.concatenate(norms, axis=0)
        update = jnp.dot(scalar, invariant[...], preferred_element_type=F32)
        update = update + jnp.dot(norm, magnitude[...], preferred_element_type=F32)
        own_rows = features[c * NA:(c + 1) * NA, :].astype(F32)
        hidden = update / (1.0 + jnp.exp(-update)) + jnp.concatenate([own_rows] * group, axis=0)
        second = jnp.dot(
            hidden.astype(BF16), later_projector[...], preferred_element_type=F32
        ).astype(BF16)
        out = lax.dot_general(w_two, second, NT, preferred_element_type=F32)
        flat = out[0:1] + out[1:2]
        return [flat[:, i * NA:(i + 1) * NA] for i in range(group)]

    def cell_sources(c):
        rows = []
        for part in range(replicas // group):
            rows.extend(layer_one(c, part))
        return jnp.concatenate(rows, axis=0) + s_one[0:1, c * NA:(c + 1) * NA]

    def force(c, before, here, after):
        window = jnp.concatenate([before, here, after, jnp.zeros_like(after)], axis=1)
        high, low = split_bf16(window)
        stacked = jnp.concatenate([high.astype(F32), low.astype(F32)], axis=0).astype(BF16)
        result = jnp.zeros((replicas, 3 * NA), F32)
        for r in range(replicas):
            out = lax.dot_general(stacked, vectors[c, r], NT, preferred_element_type=F32)
            result = jnp.where(replica_row == r, out[:replicas] + out[replicas:], result)
        return result

    order = [0] if cells == 1 else [0, cells - 1] + list(range(1, cells - 1))

    def step(t, carry):
        moving = jnp.where(t > 0, 1.0, 0.0).astype(F32)
        places_now, half_speeds = [], []
        for d in range(3):
            half = state_v[d] + (0.5 * step_time) * state_g[d]
            x = state_x[d] + (moving * step_time) * half
            state_x[d] = x
            half_speeds.append(half[:, :own])
            if d == 2:
                x = x + shift
            places_now.append(x)
        for c in range(cells):
            for d in range(3):
                x = places_now[d]
                pieces = [x[:, at:at + NA] for at in (cell_at(c - 1), cell_at(c), cell_at(c + 1))]
                win[c, d, :, :] = jnp.concatenate(pieces + pieces[2:], axis=1)
        tall = jnp.concatenate(places_now, axis=0)
        for at in range(0, own, LANES):
            columns[at:at + LANES, 0:3 * replicas] = tall[:, at:at + LANES].T

        sources = {}
        sent = []

        def send_sources():
            s_send[t] = jnp.concatenate([sources[0], sources[cells - 1]], axis=1)
            sent.append(remote(s_send.at[t], s_recv.at[t, 1], s_send_sem.at[t, 0], s_recv_sem.at[t, 0], left))
            sent.append(remote(s_send.at[t], s_recv.at[t, 0], s_send_sem.at[t, 1], s_recv_sem.at[t, 1], right))
            for copy in sent:
                copy.start()

        for c in order:
            sources[c] = cell_sources(c)
            if not sent and 0 in sources and cells - 1 in sources:
                send_sources()
        forces = {}
        for c in order[2:]:
            forces[c] = force(c, sources[c - 1], sources[c], sources[c + 1])
        for copy in sent:
            copy.wait()
        sources[-1] = s_recv[t, 0, :, NA:2 * NA]
        sources[cells] = s_recv[t, 1, :, 0:NA]
        for c in order[:2]:
            forces[c] = force(c, sources[c - 1], sources[c], sources[c + 1])

        kinetic = jnp.zeros((replicas, 1), F32)
        pushes, quick = [], []
        for d in range(3):
            g = jnp.concatenate([forces[c][:, d * NA:(d + 1) * NA] for c in range(cells)], axis=1)
            v = half_speeds[d] + (moving * (0.5 * step_time)) * g
            vg_send[t, 0, d, :, :] = jnp.concatenate([v[:, :NA], g[:, :NA]], axis=1)
            vg_send[t, 1, d, :, :] = jnp.concatenate([v[:, own - NA:], g[:, own - NA:]], axis=1)
            kinetic = kinetic + jnp.sum(v * v, axis=1, keepdims=True)
            pushes.append(g)
            quick.append(v)
        across = jnp.sum(jnp.where(diagonal, kinetic, 0.0), axis=0, keepdims=True)
        kin_send[t] = across
        kin_recv[t, n - 1] = across

        def spread(d, inner):
            remote(
                kin_send.at[t], kin_recv.at[t, d - 1], kin_send_sem.at[t], kin_recv_sem.at[t],
                lax.rem(me + d, n),
            ).start()
            return inner

        lax.fori_loop(1, n, spread, 0)
        swaps = [
            remote(vg_send.at[t, 0], vg_recv.at[t, 1], vg_send_sem.at[t, 0], vg_recv_sem.at[t, 0], left),
            remote(vg_send.at[t, 1], vg_recv.at[t, 0], vg_send_sem.at[t, 1], vg_recv_sem.at[t, 1], right),
        ]
        for copy in swaps:
            copy.start()
        everything = kin_recv.at[t, pl.ds(0, n - 1)]
        pltpu.make_async_copy(everything, everything, kin_send_sem.at[t]).wait()
        pltpu.make_async_copy(everything, everything, kin_recv_sem.at[t]).wait()
        for copy in swaps:
            copy.wait()
        collected = jnp.sum(kin_recv[t], axis=0)
        gathered = jnp.sum(
            jnp.where(diagonal, collected, 0.0), axis=1, keepdims=True
        )
        stretch = jnp.sqrt(target / (gathered / (3.0 * own * n) + motion_work_lower_limit))
        stretch = jnp.where(t > 0, stretch, 1.0)
        rest = jnp.zeros((replicas, width - own - 2 * NA), F32)
        for d in range(3):
            from_left, from_right = vg_recv[t, 0, d], vg_recv[t, 1, d]
            state_v[d] = stretch * jnp.concatenate(
                [quick[d], from_right[:, :NA], from_left[:, :NA], rest], axis=1
            )
            state_g[d] = jnp.concatenate(
                [pushes[d], from_right[:, NA:], from_left[:, NA:], rest], axis=1
            )
        return carry

    lax.fori_loop(0, STEPS + 1, step, 0)

    def pick(values):
        result = jnp.zeros_like(values)
        for r in range(replicas):
            result = jnp.where(source == r, values[r:r + 1], result)
        return result

    heat = jnp.sqrt(target / pick(target))
    floor = (
        me * cells + lax.broadcasted_iota(jnp.int32, (1, own), 1) // NA
    ).astype(F32)
    for d in range(3):
        x = pick(state_x[d][:, :own])
        if d == 2:
            x = x - floor
        places_out[:, d, :] = x
        speeds_out[:, d, :] = pick(state_v[d][:, :own]) * heat
        forces_out[:, d, :] = pick(state_g[d][:, :own])


def on_device(
    particle_places,
    particle_speeds,
    thermal_targets,
    element_features,
    swap_counterpart_slot,
    swap_approval_flags,
    initial_signal_projector,
    initial_distance_filter,
    initial_directional_scales,
    invariant_revision_matrix,
    magnitude_revision_matrix,
    later_signal_projector,
    later_directional_scales,
    push_output_matrix,
):
    n = lax.axis_size("dom")
    replicas, _, own = particle_places.shape
    cells = own // NA
    channels = element_features.shape[1]
    width = -(-(own + 2 * NA) // LANES) * LANES
    padded = -(-own // LANES) * LANES
    rounds = STEPS + 1
    group = min(4, replicas)
    basis = initial_distance_filter.shape[0]
    depth = basis * 3 * NA
    vmem = pl.BlockSpec(memory_space=pltpu.VMEM)
    smem = pl.BlockSpec(memory_space=pltpu.SMEM)
    out = jax.ShapeDtypeStruct(particle_places.shape, F32)
    return pl.pallas_call(
        functools.partial(kernel, n, replicas, cells, group),
        out_shape=(out, out, out),
        in_specs=[vmem, vmem, smem, smem, smem] + [vmem] * 9,
        out_specs=(vmem, vmem, vmem),
        scratch_shapes=[
            pltpu.VMEM((2, NA, channels), BF16),
            pltpu.VMEM((3, replicas, LANES), F32),
            pltpu.VMEM((2, 3, replicas, LANES), F32),
            pltpu.VMEM((cells, depth, channels), BF16),
            pltpu.VMEM((cells, 4 * NA, channels), BF16),
            pltpu.VMEM((1, width), F32),
            pltpu.VMEM((3, replicas, width), F32),
            pltpu.VMEM((3, replicas, width), F32),
            pltpu.VMEM((3, replicas, width), F32),
            pltpu.VMEM((cells, 3, replicas, 2 * LANES), F32),
            pltpu.VMEM((padded, 3 * replicas), F32),
            pltpu.VMEM((replicas * NA, depth), BF16),
            pltpu.VMEM((cells, replicas, 3 * NA, 2 * LANES), BF16),
            pltpu.VMEM((replicas, width), F32),
            pltpu.VMEM((rounds, replicas, LANES), F32),
            pltpu.VMEM((rounds, 2, replicas, LANES), F32),
            pltpu.VMEM((rounds, 2, 3, replicas, LANES), F32),
            pltpu.VMEM((rounds, 2, 3, replicas, LANES), F32),
            pltpu.VMEM((rounds, 1, LANES), F32),
            pltpu.VMEM((rounds, n, 1, LANES), F32),
            pltpu.SemaphoreType.DMA((4,)),
            pltpu.SemaphoreType.DMA((4,)),
            pltpu.SemaphoreType.DMA((rounds, 2)),
            pltpu.SemaphoreType.DMA((rounds, 2)),
            pltpu.SemaphoreType.DMA((rounds, 2)),
            pltpu.SemaphoreType.DMA((rounds, 2)),
            pltpu.SemaphoreType.DMA((rounds,)),
            pltpu.SemaphoreType.DMA((rounds,)),
        ],
        compiler_params=pltpu.CompilerParams(
            collective_id=0, has_side_effects=True, vmem_limit_bytes=48 * 1024 * 1024
        ),
    )(
        particle_places,
        particle_speeds,
        thermal_targets,
        swap_counterpart_slot,
        swap_approval_flags,
        element_features,
        initial_signal_projector,
        initial_distance_filter,
        initial_directional_scales.reshape(1, -1),
        invariant_revision_matrix,
        magnitude_revision_matrix,
        later_signal_projector,
        later_directional_scales.reshape(1, -1),
        push_output_matrix.reshape(1, -1),
    )


def solution(mesh):
    along = P("groups", None, "dom")
    return jax.shard_map(
        on_device,
        mesh=mesh,
        in_specs=(
            along,
            along,
            P("groups"),
            P(("groups", "dom"), None),
            P("groups"),
            P("groups"),
            P(),
            P(),
            P(),
            P(),
            P(),
            P(),
            P(),
            P(),
        ),
        out_specs=(along, along, along),
        check_vma=False,
    )
```

time: 300 us -> 83.9 us (0.28)
  blocking collectives: 136 us -> 0 us
  Pallas kernels: 0 us -> 75.8 us
  starting transfers between devices: 51 us -> 0 us
  other arithmetic: 46 us -> 0 us
  matrix products: 39.7 us -> 0 us
  waiting for transfers between devices: 18.7 us -> 0 us
    psum x4 -> x0, blocking collectives: 136 us -> none  [on_device(): lax.psum(jnp.sum(speed_entry * speed_entry, axis=(1, 2)), 'dom')]
    pallas_call x0 -> x1, Pallas kernels: none -> 75.8 us  [on_device(): pl.pallas_call(functools.partial(kernel, n, replicas, cells, group), out_...]
    ppermute x22 -> x0, starting transfers between devices: 51 us -> none  [the longest x11 49.8 us: with_halo(): lax.ppermute(head, axis, [((i + 1) % count, i) for i in range(count)])]
    dot_general x26 -> x0, matrix products: 39.7 us -> none  [the longest x5 25.2 us: layer_one(): jnp.einsum('vyegd,ydm->vyegm', single_row_count, exchange_mate, preferred...]
    another operation x10 -> x0, other arithmetic: 31.5 us -> none
    ppermute x22 -> x0, waiting for transfers between devices: 18.7 us -> none  [the longest x11 18.3 us: with_halo(): lax.ppermute(tail, axis, [(i, (i + 1) % count) for i in range(count)])]
    reduce_sum x21 -> x0, other arithmetic: 10.1 us -> none  [the longest x5 3.86 us: layer_one(): jnp.sum(reduced_sum[:, :, :, :basis_count] * initial_distance_filter, axi...]
  transfers between devices with their start and end apart: 22 -> 0, of which waited for: 10 -> 0; matrix products, arithmetic and copies ran while one was open for 4% -> 0% of each run, Pallas kernels for 0% -> 0%
where the time goes in v1:
time: 83.9 us; the launch traced here: 83.5 us
  Pallas kernels  75.8 us (90%)
  local copies, waits for them, and re-layouts  6.9 us (8%)
    pallas_call x1, Pallas kernels, on_device(): pl.pallas_call(functools.partial(kernel, n, replicas, cells, group), out_...  75.8 us
    unnamed x26, local copies, waits for them, and re-layouts  5.06 us
    pallas_call x3, local copies, waits for them, and re-layouts, on_device(): pl.pallas_call(functools.partial(kernel, n, replicas, cells, group), out_...  1.84 us

profile of v1, /device:TPU:0, one launch (start us, length us, event | category | flops | bytes accessed | tf_op | source)
XLA Modules:
  0.0 83.5 jit_solution(8637311374007363105)
XLA Ops:
  0.6 0.0 copy-start.5
  0.6 0.0 copy-start.6
  0.7 0.0 copy-start.7
  0.7 0.0 copy-start.8
  0.7 0.0 copy-start
  0.7 0.0 copy-start.2
  0.7 0.8 copy.17.places
  1.5 0.0 copy-start.1
  1.5 0.8 copy.18.speeds
  2.3 0.0 copy-done.5
  2.3 0.0 copy-done.6
  2.3 0.0 copy-done.7
  2.3 0.0 copy-done.8
  2.3 0.0 copy-done
  2.3 0.0 copy-done.2
  2.3 0.0 copy-done.1
  2.3 0.0 copy-start.3
  2.3 0.7 copy-done.3
  3.1 0.0 copy-start.4
  3.1 0.8 copy-done.4
  3.9 0.0 copy-start.9
  3.9 0.7 copy-done.9
  4.5 0.0 copy-start.10
  4.5 0.7 copy-done.10
  5.2 0.0 copy-start.11
  5.2 0.7 copy-done.11
  5.8 75.8 %shard_map.157 = (f32[8,3,192]{2,1,0:T(4,128)S(1)}, f32[8,3,192]{2,1,0:T(4,128)S(1)}, f32[8,3,192]{2,1,0:T(4,128)S(1)}) custom-call(f32[8,3,192]{2,1,0:T(4,128)S(1)} %copy.17.places, f32[8,3,192]{2,1,0:T(4,128)S(1)} %copy.18.speeds, f32[8]{0:T(128)S(1)} %copy-done.6, s32[8]{0:T(128)S(1)} %copy-done.7, s32[8]{0:T(128)S(1)} %copy-done.8, ...), custom_call_target="tpu_custom_call" | custom-call | tf_op jit(solution)/shard_map/pallas_call | solution.py:391
  81.7 0.6 copy.19
  82.3 0.6 copy.20
  82.9 0.6 copy.21
Async XLA Ops:
  0.6 1.6 %copy-start.5 = (f32[8,128]{1,0:T(8,128)S(1)}, f32[8,128]{1,0:T(8,128)}, u32[]{:S(2)}) copy-start(f32[8,128]{1,0:T(8,128)} %radial_filter.1) | copy-start | bytes 12292
  0.6 1.6 %copy-start.6 = (f32[8]{0:T(128)S(1)}, f32[8]{0:T(128)}, u32[]{:S(2)}) copy-start(f32[8]{0:T(128)} %targets.1) | copy-start | bytes 100
  0.7 1.6 %copy-start.7 = (s32[8]{0:T(128)S(1)}, s32[8]{0:T(128)}, u32[]{:S(2)}) copy-start(s32[8]{0:T(128)} %slots.1) | copy-start | bytes 100
  0.7 1.6 %copy-start.8 = (s32[8]{0:T(128)S(1)}, s32[8]{0:T(128)}, u32[]{:S(2)}) copy-start(s32[8]{0:T(128)} %flags.1) | copy-start | bytes 100
  0.7 1.6 %copy-start = (bf16[192,128]{1,0:T(8,128)(2,1)S(1)}, bf16[192,128]{1,0:T(8,128)(2,1)}, u32[]{:S(2)}) copy-start(bf16[192,128]{1,0:T(8,128)(2,1)} %features.1) | copy-start | bytes 147460
  0.7 1.6 %copy-start.2 = (bf16[128,128]{1,0:T(8,128)(2,1)S(1)}, bf16[128,128]{1,0:T(8,128)(2,1)}, u32[]{:S(2)}) copy-start(bf16[128,128]{1,0:T(8,128)(2,1)} %invariant.1) | copy-start | bytes 98308
  1.5 0.8 copy-start.1
  2.3 0.8 copy-start.3
  3.1 0.8 copy-start.4
  3.9 0.7 copy-start.9
  4.5 0.7 copy-start.10
  5.2 0.7 copy-start.11

commit v2 on v1

v2 whole, which is shorter than its diff:
```python
import functools
import math

import jax
import jax.numpy as jnp
from jax import lax
from jax.experimental import pallas as pl
from jax.experimental.pallas import tpu as pltpu
from jax.sharding import PartitionSpec as P

NA = 64
STEPS = 4
LANES = 128
CHUNK = 16
LOG2E = math.log2(math.e)

step_time = 0.05
motion_work_lower_limit = 1e-06

F32 = jnp.float32
BF16 = jnp.bfloat16
MESH = pl.DeviceIdType.MESH
NT = (((1,), (1,)), ((), ()))


def split_bf16(values):
    high = values.astype(BF16)
    low = (values - high.astype(F32)).astype(BF16)
    return high, low


def weight_rows(weights):
    high, low = split_bf16(weights)
    high, low = high.astype(F32), low.astype(F32)
    row = lax.broadcasted_iota(jnp.int32, (16, weights.shape[1]), 0)
    return jnp.where(row == 0, high, jnp.where(row == 1, low, 0.0)).astype(BF16)


def pair_base(rows, columns):
    dx, dy, dz = [row - column for row, column in zip(rows, columns)]
    squared = dx * dx + dy * dy + dz * dz
    inside = jnp.maximum(1.0 - squared, 0.0)
    envelope = inside * inside
    centered = 0.5 - inside
    base = jnp.exp2((centered * centered) * (-98.0 * LOG2E)) * envelope
    return (dx * envelope, dy * envelope, dz * envelope), base, centered


def kernel(
    n, replicas, cells, parts,
    places, speeds, targets, slots, flags, features,
    projector, radial_filter, scales_one, invariant, magnitude, later_projector, scales_two, push,
    places_out, speeds_out, forces_out,
    feature_halo, place_send, place_halo, table_one, table_vec, s_one,
    state_x, state_v, state_g, win, columns, vectors,
    s_send, s_recv, vg_send, vg_recv, kin_send, kin_recv,
    init_send_sem, init_recv_sem, s_send_sem, s_recv_sem, vg_send_sem, vg_recv_sem,
    kin_send_sem, kin_recv_sem,
):
    me = lax.axis_index("dom")
    left = lax.rem(me + n - 1, n)
    right = lax.rem(me + 1, n)
    own = cells * NA
    width = state_x.shape[3]
    group = replicas // parts
    right_at, left_at = own, own + NA
    channels = features.shape[1]

    def cell_at(c):
        return left_at if c < 0 else c * NA

    barrier = pltpu.get_barrier_semaphore()

    def greet(d, carry):
        pl.semaphore_signal(barrier, inc=1, device_id={"dom": lax.rem(me + d, n)}, device_id_type=MESH)
        return carry

    lax.fori_loop(1, n, greet, 0)

    zeros_pad = jnp.zeros((group, width - own), F32)
    for d in range(3):
        x = places[d]
        place_send[d] = jnp.concatenate([x[:, :NA], x[:, own - NA:]], axis=1)
        for p in range(parts):
            members = slice(p * group, (p + 1) * group)
            state_x[p, d] = jnp.concatenate([x[members], zeros_pad], axis=1)
            state_v[p, d] = jnp.concatenate([speeds[d, members, :], zeros_pad], axis=1)
            state_g[p, d] = jnp.zeros((group, width), F32)

    pl.semaphore_wait(barrier, n - 1)

    def remote(src, dst, send_sem, recv_sem, to):
        return pltpu.make_async_remote_copy(
            src_ref=src, dst_ref=dst, send_sem=send_sem, recv_sem=recv_sem,
            device_id={"dom": to}, device_id_type=MESH,
        )

    first = [
        remote(place_send, place_halo.at[1], init_send_sem.at[0], init_recv_sem.at[0], left),
        remote(place_send, place_halo.at[0], init_send_sem.at[1], init_recv_sem.at[1], right),
        remote(features.at[pl.ds(0, NA)], feature_halo.at[1], init_send_sem.at[2], init_recv_sem.at[2], left),
        remote(features.at[pl.ds(own - NA, NA)], feature_halo.at[0], init_send_sem.at[3], init_recv_sem.at[3], right),
    ]
    for copy in first:
        copy.start()

    basis = radial_filter.shape[0]
    offset = lax.broadcasted_iota(jnp.int32, radial_filter.shape, 0).astype(F32) - 0.5 * (basis - 1)
    filters = radial_filter[...] * jnp.exp(-2.0 * offset * offset)
    push_row = push[...]
    w_one = weight_rows(scales_one[...] * push_row)
    w_two = weight_rows(scales_two[...] * push_row)
    scale_row = scales_one[...] * scales_one[...]

    def make_table(rows):
        return jnp.dot(rows, projector[...], preferred_element_type=F32).astype(BF16)

    tables = {c: make_table(features[c * NA:(c + 1) * NA, :]) for c in range(cells)}
    for copy in first:
        copy.wait()
    tables[-1] = make_table(feature_halo[0])
    tables[cells] = make_table(feature_halo[1])

    s_parts = []
    for c in list(range(cells)) + [cells, -1]:
        out = lax.dot_general(w_one, tables[c], NT, preferred_element_type=F32)
        s_parts.append(out[0:1] + out[1:2])
    s_one[...] = jnp.concatenate(s_parts + [jnp.zeros((1, width - own - 2 * NA), F32)], axis=1)

    for c in range(cells):
        before, here, after = [tables[c + j].astype(F32) for j in (-1, 0, 1)]
        table_vec[c, 0:NA, :] = tables[c - 1]
        table_vec[c, NA:2 * NA, :] = tables[c]
        table_vec[c, 2 * NA:3 * NA, :] = tables[c + 1]
        table_vec[c, 3 * NA:4 * NA, :] = jnp.zeros((NA, channels), BF16)
        for k in range(8):
            row = filters[k:k + 1]
            table_one[c, k * LANES:k * LANES + NA, :] = (before * row).astype(BF16)
            table_one[c, k * LANES + NA:(k + 1) * LANES, :] = (here * row).astype(BF16)
        for j in range(4):
            at = (8 + j) * LANES
            table_one[c, at:at + NA, :] = (after * filters[4 + j:5 + j]).astype(BF16)
            table_one[c, at + NA:at + LANES, :] = (after * filters[3 - j:4 - j]).astype(BF16)

    for d in range(3):
        for p in range(parts):
            members = slice(p * group, (p + 1) * group)
            state_x[p, d, :, right_at:right_at + NA] = place_halo[1, d, members, 0:NA]
            state_x[p, d, :, left_at:left_at + NA] = place_halo[0, d, members, NA:2 * NA]

    total = float(cells * n)
    lane = lax.broadcasted_iota(jnp.int32, (1, width), 1)
    up = jnp.where(me == n - 1, total, 0.0).astype(F32)
    down = jnp.where(me == 0, -total, 0.0).astype(F32)
    shift = jnp.where(
        (lane >= right_at) & (lane < right_at + NA), up,
        jnp.where((lane >= left_at) & (lane < left_at + NA), down, 0.0),
    )
    side = jnp.where(lax.broadcasted_iota(jnp.int32, (1, LANES), 1) < NA, 14.0 * LOG2E, -14.0 * LOG2E).astype(F32)
    member_row = lax.broadcasted_iota(jnp.int32, (group, 1), 0)
    replica_row = lax.broadcasted_iota(jnp.int32, (replicas, 1), 0)
    diagonal = (
        lax.broadcasted_iota(jnp.int32, (group, LANES), 0)
        == lax.broadcasted_iota(jnp.int32, (group, LANES), 1)
    )
    target = jnp.zeros((replicas, 1), F32)
    source = jnp.zeros((replicas, 1), jnp.int32)
    for r in range(replicas):
        target = jnp.where(replica_row == r, targets[r], target)
        source = jnp.where(replica_row == r, jnp.where(flags[r] > 0, slots[r], r), source)

    def chain(start, power):
        values = [start]
        for _ in range(3):
            values.append(values[-1] * power)
        return values

    def build(p, c, r):
        rows = [win[p, c, d, r:r + 1, :] for d in range(3)]
        tall = []
        for at in range(0, NA, CHUNK):
            out = slice(at, at + CHUNK)
            cols = [
                columns[p, c * NA + at:c * NA + at + CHUNK, d * group + r:d * group + r + 1]
                for d in range(3)
            ]
            cols = [jnp.broadcast_to(col, (CHUNK, LANES)) for col in cols]
            vec, base, t = pair_base([row[:, :LANES] for row in rows], cols)
            for d in range(3):
                vectors[p, c, r, d * NA + at:d * NA + at + CHUNK, 0:LANES] = vec[d].astype(BF16)
            grow = jnp.exp2((14.0 * LOG2E) * t)
            shrink = jnp.exp2((-14.0 * LOG2E) * t)
            high = chain(base * grow, grow * grow)
            low = chain(base * shrink, shrink * shrink)
            vec, base, t = pair_base([row[:, LANES:] for row in rows], cols)
            for d in range(3):
                vectors[p, c, r, d * NA + at:d * NA + at + CHUNK, LANES:] = vec[d].astype(BF16)
            grow = jnp.exp2(side * t)
            both = chain(base * grow, grow * grow)
            tall.append([x.astype(BF16) for x in low[::-1] + high + both])
        wide = [jnp.concatenate([part[k] for part in tall], axis=0) for k in range(12)]
        return jnp.concatenate(wide, axis=1)

    def layer_one(p, c):
        gauss = jnp.concatenate([build(p, c, r) for r in range(group)], axis=0)
        scalar = jnp.dot(gauss, table_one[c], preferred_element_type=F32).astype(BF16)
        norms = []
        for r in range(group):
            vec = jnp.dot(vectors[p, c, r], table_vec[c], preferred_element_type=F32)
            one, two, three = [vec[d * NA:(d + 1) * NA] for d in range(3)]
            norms.append(((one * one + two * two + three * three) * scale_row).astype(BF16))
        norm = jnp.concatenate(norms, axis=0)
        update = jnp.dot(scalar, invariant[...], preferred_element_type=F32)
        update = update + jnp.dot(norm, magnitude[...], preferred_element_type=F32)
        own_rows = features[c * NA:(c + 1) * NA, :].astype(F32)
        half = 0.5 * update
        hidden = half * jnp.tanh(half) + half + jnp.concatenate([own_rows] * group, axis=0)
        second = jnp.dot(
            hidden.astype(BF16), later_projector[...], preferred_element_type=F32
        ).astype(BF16)
        out = lax.dot_general(w_two, second, NT, preferred_element_type=F32)
        flat = out[0:1] + out[1:2]
        rows = [flat[:, i * NA:(i + 1) * NA] for i in range(group)]
        return jnp.concatenate(rows, axis=0) + s_one[0:1, c * NA:(c + 1) * NA]

    def force(p, c, before, here, after):
        window = jnp.concatenate([before, here, after, jnp.zeros_like(after)], axis=1)
        high, low = split_bf16(window)
        stacked = jnp.concatenate([high.astype(F32), low.astype(F32)] * 2, axis=0).astype(BF16)
        result = jnp.zeros((group, 3 * NA), F32)
        for r in range(group):
            out = lax.dot_general(stacked, vectors[p, c, r], NT, preferred_element_type=F32)
            result = jnp.where(member_row == r, out[:group] + out[group:2 * group], result)
        return result

    order = [0] if cells == 1 else [0, cells - 1] + list(range(1, cells - 1))

    def is_moving(t):
        return jnp.where(t > 0, 1.0, 0.0).astype(F32)

    def s_copies(t, p):
        return [
            remote(s_send.at[t, p], s_recv.at[t, p, 1], s_send_sem.at[t, p, 0], s_recv_sem.at[t, p, 0], left),
            remote(s_send.at[t, p], s_recv.at[t, p, 0], s_send_sem.at[t, p, 1], s_recv_sem.at[t, p, 1], right),
        ]

    def vg_copies(t, p):
        return [
            remote(vg_send.at[t, p, 0], vg_recv.at[t, p, 1], vg_send_sem.at[t, p, 0], vg_recv_sem.at[t, p, 0], left),
            remote(vg_send.at[t, p, 1], vg_recv.at[t, p, 0], vg_send_sem.at[t, p, 1], vg_recv_sem.at[t, p, 1], right),
        ]

    def first_half(t, p):
        moving = is_moving(t)
        places_now = []
        for d in range(3):
            half = state_v[p, d] + (0.5 * step_time) * state_g[p, d]
            x = state_x[p, d] + (moving * step_time) * half
            state_v[p, d] = half
            state_x[p, d] = x
            if d == 2:
                x = x + shift
            places_now.append(x)
        for c in range(cells):
            for d in range(3):
                x = places_now[d]
                pieces = [x[:, at:at + NA] for at in (cell_at(c - 1), cell_at(c), cell_at(c + 1))]
                win[p, c, d, :, :] = jnp.concatenate(pieces + pieces[2:], axis=1)
        tall = jnp.concatenate(places_now + [jnp.zeros((-3 * group % 8, width), F32)], axis=0)
        for at in range(0, own, LANES):
            columns[p, at:at + LANES, :] = tall[:, at:at + LANES].T
        sources = {}
        sent = False
        for c in order:
            sources[c] = layer_one(p, c)
            if not sent and 0 in sources and cells - 1 in sources:
                sent = True
                s_send[t, p] = jnp.concatenate([sources[0], sources[cells - 1]], axis=1)
                for copy in s_copies(t, p):
                    copy.start()
        return sources

    def second_half(t, p, sources):
        moving = is_moving(t)
        forces = {}
        for c in order[2:]:
            forces[c] = force(p, c, sources[c - 1], sources[c], sources[c + 1])
        for copy in s_copies(t, p):
            copy.wait()
        sources[-1] = s_recv[t, p, 0, :, NA:2 * NA]
        sources[cells] = s_recv[t, p, 1, :, 0:NA]
        for c in order[:2]:
            forces[c] = force(p, c, sources[c - 1], sources[c], sources[c + 1])
        kinetic = jnp.zeros((group, 1), F32)
        for d in range(3):
            g = jnp.concatenate([forces[c][:, d * NA:(d + 1) * NA] for c in range(cells)], axis=1)
            v = state_v[p, d, :, 0:own] + (moving * (0.5 * step_time)) * g
            vg_send[t, p, 0, d] = jnp.concatenate([v[:, :NA], g[:, :NA]], axis=1)
            vg_send[t, p, 1, d] = jnp.concatenate([v[:, own - NA:], g[:, own - NA:]], axis=1)
            kinetic = kinetic + jnp.sum(v * v, axis=1, keepdims=True)
            state_v[p, d, :, 0:own] = v
            state_g[p, d, :, 0:own] = g
        across = jnp.sum(jnp.where(diagonal, kinetic, 0.0), axis=0, keepdims=True)
        kin_send[t, p] = across
        kin_recv[t, p, n - 1] = across

        def spread(d, inner):
            remote(
                kin_send.at[t, p], kin_recv.at[t, p, d - 1], kin_send_sem.at[t, p],
                kin_recv_sem.at[t, p], lax.rem(me + d, n),
            ).start()
            return inner

        lax.fori_loop(1, n, spread, 0)
        for copy in vg_copies(t, p):
            copy.start()

    def finish(t, p):
        everything = kin_recv.at[t, p, pl.ds(0, n - 1)]
        for copy in vg_copies(t, p):
            copy.wait()
        pltpu.make_async_copy(everything, everything, kin_send_sem.at[t, p]).wait()
        pltpu.make_async_copy(everything, everything, kin_recv_sem.at[t, p]).wait()
        collected = jnp.sum(kin_recv[t, p], axis=0)
        gathered = jnp.sum(jnp.where(diagonal, collected, 0.0), axis=1, keepdims=True)
        goal = target[p * group:(p + 1) * group]
        stretch = jnp.sqrt(goal / (gathered / (3.0 * own * n) + motion_work_lower_limit))
        stretch = jnp.where(t > 0, stretch, 1.0)
        rest = jnp.zeros((group, width - own - 2 * NA), F32)
        for d in range(3):
            from_left, from_right = vg_recv[t, p, 0, d], vg_recv[t, p, 1, d]
            state_v[p, d] = stretch * jnp.concatenate(
                [state_v[p, d, :, 0:own], from_right[:, :NA], from_left[:, :NA], rest], axis=1
            )
            state_g[p, d, :, right_at:right_at + NA] = from_right[:, NA:]
            state_g[p, d, :, left_at:left_at + NA] = from_left[:, NA:]

    def step(t, carry):
        sources = []
        for p in range(parts):
            pl.when(t > 0)(functools.partial(finish, t - 1, p))
            sources.append(first_half(t, p))
        for p in range(parts):
            second_half(t, p, sources[p])
        return carry

    lax.fori_loop(0, STEPS + 1, step, 0)
    for p in range(parts):
        finish(STEPS, p)

    def pick(values):
        result = jnp.zeros_like(values)
        for r in range(replicas):
            result = jnp.where(source == r, values[r:r + 1], result)
        return result

    def whole(state, d):
        return jnp.concatenate([state[p, d, :, 0:own] for p in range(parts)], axis=0)

    heat = jnp.sqrt(target / pick(target))
    floor = (
        me * cells + lax.broadcasted_iota(jnp.int32, (1, own), 1) // NA
    ).astype(F32)
    for d in range(3):
        x = pick(whole(state_x, d))
        if d == 2:
            x = x - floor
        places_out[d] = x
        speeds_out[d] = pick(whole(state_v, d)) * heat
        forces_out[d] = pick(whole(state_g, d))


def on_device(
    particle_places,
    particle_speeds,
    thermal_targets,
    element_features,
    swap_counterpart_slot,
    swap_approval_flags,
    initial_signal_projector,
    initial_distance_filter,
    initial_directional_scales,
    invariant_revision_matrix,
    magnitude_revision_matrix,
    later_signal_projector,
    later_directional_scales,
    push_output_matrix,
):
    n = lax.axis_size("dom")
    replicas, _, own = particle_places.shape
    cells = own // NA
    channels = element_features.shape[1]
    width = -(-(own + 2 * NA) // LANES) * LANES
    padded = -(-own // LANES) * LANES
    rounds = STEPS + 1
    parts = 2 if replicas % 2 == 0 else 1
    group = replicas // parts
    pad_rows = -(-3 * group // 8) * 8
    basis = initial_distance_filter.shape[0]
    depth = basis * 3 * NA
    vmem = pl.BlockSpec(memory_space=pltpu.VMEM)
    smem = pl.BlockSpec(memory_space=pltpu.SMEM)
    out = jax.ShapeDtypeStruct((3, replicas, own), F32)
    results = pl.pallas_call(
        functools.partial(kernel, n, replicas, cells, parts),
        out_shape=(out, out, out),
        in_specs=[vmem, vmem, smem, smem, smem] + [vmem] * 9,
        out_specs=(vmem, vmem, vmem),
        scratch_shapes=[
            pltpu.VMEM((2, NA, channels), BF16),
            pltpu.VMEM((3, replicas, LANES), F32),
            pltpu.VMEM((2, 3, replicas, LANES), F32),
            pltpu.VMEM((cells, depth, channels), BF16),
            pltpu.VMEM((cells, 4 * NA, channels), BF16),
            pltpu.VMEM((1, width), F32),
            pltpu.VMEM((parts, 3, group, width), F32),
            pltpu.VMEM((parts, 3, group, width), F32),
            pltpu.VMEM((parts, 3, group, width), F32),
            pltpu.VMEM((parts, cells, 3, group, 2 * LANES), F32),
            pltpu.VMEM((parts, padded, pad_rows), F32),
            pltpu.VMEM((parts, cells, group, 3 * NA, 2 * LANES), BF16),
            pltpu.VMEM((rounds, parts, group, LANES), F32),
            pltpu.VMEM((rounds, parts, 2, group, LANES), F32),
            pltpu.VMEM((rounds, parts, 2, 3, group, LANES), F32),
            pltpu.VMEM((rounds, parts, 2, 3, group, LANES), F32),
            pltpu.VMEM((rounds, parts, 1, LANES), F32),
            pltpu.VMEM((rounds, parts, n, 1, LANES), F32),
            pltpu.SemaphoreType.DMA((4,)),
            pltpu.SemaphoreType.DMA((4,)),
            pltpu.SemaphoreType.DMA((rounds, parts, 2)),
            pltpu.SemaphoreType.DMA((rounds, parts, 2)),
            pltpu.SemaphoreType.DMA((rounds, parts, 2)),
            pltpu.SemaphoreType.DMA((rounds, parts, 2)),
            pltpu.SemaphoreType.DMA((rounds, parts)),
            pltpu.SemaphoreType.DMA((rounds, parts)),
        ],
        compiler_params=pltpu.CompilerParams(
            collective_id=0, has_side_effects=True, vmem_limit_bytes=48 * 1024 * 1024
        ),
    )(
        jnp.transpose(particle_places, (1, 0, 2)),
        jnp.transpose(particle_speeds, (1, 0, 2)),
        thermal_targets,
        swap_counterpart_slot,
        swap_approval_flags,
        element_features,
        initial_signal_projector,
        initial_distance_filter,
        initial_directional_scales.reshape(1, -1),
        invariant_revision_matrix,
        magnitude_revision_matrix,
        later_signal_projector,
        later_directional_scales.reshape(1, -1),
        push_output_matrix.reshape(1, -1),
    )
    return tuple(jnp.transpose(result, (1, 0, 2)) for result in results)


def solution(mesh):
    along = P("groups", None, "dom")
    return jax.shard_map(
        on_device,
        mesh=mesh,
        in_specs=(
            along,
            along,
            P("groups"),
            P(("groups", "dom"), None),
            P("groups"),
            P("groups"),
            P(),
            P(),
            P(),
            P(),
            P(),
            P(),
            P(),
            P(),
        ),
        out_specs=(along, along, along),
        check_vma=False,
    )
```

time: 83.9 us -> 80.3 us (0.957)
  Pallas kernels: 75.8 us -> 71.1 us
  local copies, waits for them, and re-layouts: 6.9 us -> 7.82 us
    pallas_call x1, Pallas kernels: 75.8 us -> 71.1 us  [on_device(): pl.pallas_call(functools.partial(kernel, n, replicas, cells, parts), out_...]
    unnamed x26 -> x31, local copies, waits for them, and re-layouts: 5.06 us -> 7.82 us
    pallas_call x3 -> x0, local copies, waits for them, and re-layouts: 1.84 us -> none  [on_device(): pl.pallas_call(functools.partial(kernel, n, replicas, cells, group), out_...]
where the time goes in v2:
time: 80.3 us; the launch traced here: 79.7 us
  Pallas kernels  71.1 us (89%)
  local copies, waits for them, and re-layouts  7.82 us (10%)
    pallas_call x1, Pallas kernels, on_device(): pl.pallas_call(functools.partial(kernel, n, replicas, cells, parts), out_...  71.1 us
    unnamed x31, local copies, waits for them, and re-layouts  7.82 us

profile of v2, /device:TPU:0, one launch (start us, length us, event | category | flops | bytes accessed | tf_op | source)
XLA Modules:
  0.0 79.7 jit_solution(4369690804673446628)
XLA Ops:
  0.6 0.0 copy-start.7
  0.6 0.0 copy-start.11
  0.7 0.0 copy-start.12
  0.7 0.0 copy-start.13
  0.7 0.0 copy-start.8
  0.7 0.0 copy-start.9
  0.7 0.0 copy-start.10
  0.7 0.6 copy-done.7
  1.3 0.0 copy-done.11
  1.3 0.0 copy-done.12
  1.3 0.0 copy-done.13
  1.3 0.0 copy-done.8
  1.4 0.0 copy-done.9
  1.4 0.0 copy-done.10
  1.4 0.0 copy-start
  1.4 0.8 copy-done
  2.2 0.0 copy-start.1
  2.2 0.8 copy-done.1
  2.9 0.0 copy-start.2
  2.9 0.8 copy-done.2
  3.7 0.0 copy-start.3
  3.7 0.8 copy-done.3
  4.5 0.0 copy-start.4
  4.5 0.8 copy-done.4
  5.2 0.0 copy-start.5
  5.2 0.7 copy-done.5
  6.0 0.0 copy-start.6
  6.0 0.7 copy-done.6
  6.7 71.1 %shard_map.157 = (f32[3,8,192]{2,1,0:T(8,128)S(1)}, f32[3,8,192]{2,1,0:T(8,128)S(1)}, f32[3,8,192]{2,1,0:T(8,128)S(1)}) custom-call(f32[3,8,192]{2,1,0:T(8,128)S(1)} %bitcast.11, f32[3,8,192]{2,1,0:T(8,128)S(1)} %bitcast.12, f32[8]{0:T(128)S(1)} %copy-done.8, s32[8]{0:T(128)S(1)} %copy-done.9, s32[8]{0:T(128)S(1)} %copy-done.10, ...), custom_call_target="tpu_custom_call" | custom-call | tf_op jit(solution)/shard_map/pallas_call | solution.py:404
  77.8 0.6 copy.20
  78.4 0.6 copy.21
  79.1 0.6 copy.22
Async XLA Ops:
  0.6 0.7 copy-start.7
  0.6 0.7 copy-start.11
  0.7 0.7 copy-start.12
  0.7 0.7 copy-start.13
  0.7 0.7 copy-start.8
  0.7 0.7 copy-start.9
  0.7 0.7 copy-start.10
  1.4 0.8 %copy-start = (bf16[192,128]{1,0:T(8,128)(2,1)S(1)}, bf16[192,128]{1,0:T(8,128)(2,1)}, u32[]{:S(2)}) copy-start(bf16[192,128]{1,0:T(8,128)(2,1)} %features.1) | copy-start | bytes 147460
  2.2 0.8 copy-start.1
  2.9 0.8 copy-start.2
  3.7 0.8 copy-start.3
  4.5 0.8 copy-start.4
  5.2 0.7 copy-start.5
  6.0 0.7 copy-start.6

commit v3 on v2

--- a/solution.py
+++ b/solution.py
@@ -47,13 +47,13 @@
 
 
 def kernel(
-    n, replicas, cells, parts,
+    n, inner, replicas, cells, parts,
     places, speeds, targets, slots, flags, features,
     projector, radial_filter, scales_one, invariant, magnitude, later_projector, scales_two, push,
     places_out, speeds_out, forces_out,
     feature_halo, place_send, place_halo, table_one, table_vec, s_one,
     state_x, state_v, state_g, win, columns, vectors,
-    s_send, s_recv, vg_send, vg_recv, kin_send, kin_recv,
+    s_send, s_recv, vg_send, vg_recv, kin_send, kin_inner, kin_outer,
     init_send_sem, init_recv_sem, s_send_sem, s_recv_sem, vg_send_sem, vg_recv_sem,
     kin_send_sem, kin_recv_sem,
 ):
@@ -63,6 +63,7 @@
     own = cells * NA
     width = state_x.shape[3]
     group = replicas // parts
+    outer = n // inner
     right_at, left_at = own, own + NA
     channels = features.shape[1]
 
@@ -71,11 +72,12 @@
 
     barrier = pltpu.get_barrier_semaphore()
 
-    def greet(d, carry):
-        pl.semaphore_signal(barrier, inc=1, device_id={"dom": lax.rem(me + d, n)}, device_id_type=MESH)
-        return carry
-
-    lax.fori_loop(1, n, greet, 0)
+    corner = me - lax.rem(me, inner)
+    inner_peers = [corner + lax.rem(me + d, inner) for d in range(1, inner)]
+    outer_peers = [lax.rem(me + d * inner, n) for d in range(1, outer)]
+    greeted = [left, right] + inner_peers + outer_peers
+    for peer in greeted:
+        pl.semaphore_signal(barrier, inc=1, device_id={"dom": peer}, device_id_type=MESH)
 
     zeros_pad = jnp.zeros((group, width - own), F32)
     for d in range(3):
@@ -87,7 +89,7 @@
             state_v[p, d] = jnp.concatenate([speeds[d, members, :], zeros_pad], axis=1)
             state_g[p, d] = jnp.zeros((group, width), F32)
 
-    pl.semaphore_wait(barrier, n - 1)
+    pl.semaphore_wait(barrier, len(greeted))
 
     def remote(src, dst, send_sem, recv_sem, to):
         return pltpu.make_async_remote_copy(
@@ -250,7 +252,7 @@
             remote(vg_send.at[t, p, 1], vg_recv.at[t, p, 0], vg_send_sem.at[t, p, 1], vg_recv_sem.at[t, p, 1], right),
         ]
 
-    def first_half(t, p):
+    def first_half(t, p, between):
         moving = is_moving(t)
         places_now = []
         for d in range(3):
@@ -278,6 +280,7 @@
                 s_send[t, p] = jnp.concatenate([sources[0], sources[cells - 1]], axis=1)
                 for copy in s_copies(t, p):
                     copy.start()
+                between()
         return sources
 
     def second_half(t, p, sources):
@@ -301,27 +304,38 @@
             state_v[p, d, :, 0:own] = v
             state_g[p, d, :, 0:own] = g
         across = jnp.sum(jnp.where(diagonal, kinetic, 0.0), axis=0, keepdims=True)
-        kin_send[t, p] = across
-        kin_recv[t, p, n - 1] = across
-
-        def spread(d, inner):
+        kin_send[t, p, 0] = across
+        kin_inner[t, p, inner - 1] = across
+        for slot, peer in enumerate(inner_peers):
             remote(
-                kin_send.at[t, p], kin_recv.at[t, p, d - 1], kin_send_sem.at[t, p],
-                kin_recv_sem.at[t, p], lax.rem(me + d, n),
+                kin_send.at[t, p, 0], kin_inner.at[t, p, slot], kin_send_sem.at[t, p, 0],
+                kin_recv_sem.at[t, p, 0], peer,
             ).start()
-            return inner
-
-        lax.fori_loop(1, n, spread, 0)
         for copy in vg_copies(t, p):
             copy.start()
 
+    def wait_all(buffer, count, t, p, stage):
+        if count > 0:
+            everything = buffer.at[t, p, pl.ds(0, count)]
+            pltpu.make_async_copy(everything, everything, kin_send_sem.at[t, p, stage]).wait()
+            pltpu.make_async_copy(everything, everything, kin_recv_sem.at[t, p, stage]).wait()
+
+    def relay(t, p):
+        wait_all(kin_inner, inner - 1, t, p, 0)
+        partial = jnp.sum(kin_inner[t, p], axis=0)
+        kin_send[t, p, 1] = partial
+        kin_outer[t, p, outer - 1] = partial
+        for slot, peer in enumerate(outer_peers):
+            remote(
+                kin_send.at[t, p, 1], kin_outer.at[t, p, slot], kin_send_sem.at[t, p, 1],
+                kin_recv_sem.at[t, p, 1], peer,
+            ).start()
+
     def finish(t, p):
-        everything = kin_recv.at[t, p, pl.ds(0, n - 1)]
         for copy in vg_copies(t, p):
             copy.wait()
-        pltpu.make_async_copy(everything, everything, kin_send_sem.at[t, p]).wait()
-        pltpu.make_async_copy(everything, everything, kin_recv_sem.at[t, p]).wait()
-        collected = jnp.sum(kin_recv[t, p], axis=0)
+        wait_all(kin_outer, outer - 1, t, p, 1)
+        collected = jnp.sum(kin_outer[t, p], axis=0)
         gathered = jnp.sum(jnp.where(diagonal, collected, 0.0), axis=1, keepdims=True)
         goal = target[p * group:(p + 1) * group]
         stretch = jnp.sqrt(goal / (gathered / (3.0 * own * n) + motion_work_lower_limit))
@@ -335,16 +349,20 @@
             state_g[p, d, :, right_at:right_at + NA] = from_right[:, NA:]
             state_g[p, d, :, left_at:left_at + NA] = from_left[:, NA:]
 
+    def later(t, action, p):
+        pl.when(t > 0)(functools.partial(action, t - 1, p))
+
     def step(t, carry):
-        sources = []
-        for p in range(parts):
-            pl.when(t > 0)(functools.partial(finish, t - 1, p))
-            sources.append(first_half(t, p))
-        for p in range(parts):
-            second_half(t, p, sources[p])
+        later(t, finish, 0)
+        sources = first_half(t, 0, lambda: later(t, relay, 1))
+        later(t, finish, 1)
+        others = first_half(t, 1, lambda: second_half(t, 0, sources))
+        relay(t, 0)
+        second_half(t, 1, others)
         return carry
 
     lax.fori_loop(0, STEPS + 1, step, 0)
+    relay(STEPS, 1)
     for p in range(parts):
         finish(STEPS, p)
 
@@ -393,7 +411,8 @@
     width = -(-(own + 2 * NA) // LANES) * LANES
     padded = -(-own // LANES) * LANES
     rounds = STEPS + 1
-    parts = 2 if replicas % 2 == 0 else 1
+    parts = 2
+    inner = max(d for d in range(1, n + 1) if n % d == 0 and d * d <= n)
     group = replicas // parts
     pad_rows = -(-3 * group // 8) * 8
     basis = initial_distance_filter.shape[0]
@@ -402,7 +421,7 @@
     smem = pl.BlockSpec(memory_space=pltpu.SMEM)
     out = jax.ShapeDtypeStruct((3, replicas, own), F32)
     results = pl.pallas_call(
-        functools.partial(kernel, n, replicas, cells, parts),
+        functools.partial(kernel, n, inner, replicas, cells, parts),
         out_shape=(out, out, out),
         in_specs=[vmem, vmem, smem, smem, smem] + [vmem] * 9,
         out_specs=(vmem, vmem, vmem),
@@ -423,16 +442,17 @@
             pltpu.VMEM((rounds, parts, 2, group, LANES), F32),
             pltpu.VMEM((rounds, parts, 2, 3, group, LANES), F32),
             pltpu.VMEM((rounds, parts, 2, 3, group, LANES), F32),
-            pltpu.VMEM((rounds, parts, 1, LANES), F32),
-            pltpu.VMEM((rounds, parts, n, 1, LANES), F32),
+            pltpu.VMEM((rounds, parts, 2, 1, LANES), F32),
+            pltpu.VMEM((rounds, parts, inner, 1, LANES), F32),
+            pltpu.VMEM((rounds, parts, n // inner, 1, LANES), F32),
             pltpu.SemaphoreType.DMA((4,)),
             pltpu.SemaphoreType.DMA((4,)),
             pltpu.SemaphoreType.DMA((rounds, parts, 2)),
             pltpu.SemaphoreType.DMA((rounds, parts, 2)),
             pltpu.SemaphoreType.DMA((rounds, parts, 2)),
             pltpu.SemaphoreType.DMA((rounds, parts, 2)),
-            pltpu.SemaphoreType.DMA((rounds, parts)),
-            pltpu.SemaphoreType.DMA((rounds, parts)),
+            pltpu.SemaphoreType.DMA((rounds, parts, 2)),
+            pltpu.SemaphoreType.DMA((rounds, parts, 2)),
         ],
         compiler_params=pltpu.CompilerParams(
             collective_id=0, has_side_effects=True, vmem_limit_bytes=48 * 1024 * 1024

time: 80.3 us -> 95.8 us (1.19)
  Pallas kernels: 71.1 us -> 86.7 us
    pallas_call x1, Pallas kernels: 71.1 us -> 86.7 us  [on_device(): pl.pallas_call(functools.partial(kernel, n, inner, replicas, cells, parts...]
where the time goes in v3:
time: 95.8 us; the launch traced here: 95.2 us
  Pallas kernels  86.7 us (91%)
  local copies, waits for them, and re-layouts  7.82 us (8%)
    pallas_call x1, Pallas kernels, on_device(): pl.pallas_call(functools.partial(kernel, n, inner, replicas, cells, parts...  86.7 us
    unnamed x31, local copies, waits for them, and re-layouts  7.82 us

profile of v3, /device:TPU:0, one launch (start us, length us, event | category | flops | bytes accessed | tf_op | source)
XLA Modules:
  0.0 95.2 jit_solution(3663214874652198734)
XLA Ops:
  0.6 0.0 copy-start.7
  0.6 0.0 copy-start.11
  0.7 0.0 copy-start.12
  0.7 0.0 copy-start.13
  0.7 0.0 copy-start.8
  0.7 0.0 copy-start.9
  0.7 0.0 copy-start.10
  0.7 0.6 copy-done.7
  1.3 0.0 copy-done.11
  1.3 0.0 copy-done.12
  1.3 0.0 copy-done.13
  1.3 0.0 copy-done.8
  1.4 0.0 copy-done.9
  1.4 0.0 copy-done.10
  1.4 0.0 copy-start
  1.4 0.8 copy-done
  2.2 0.0 copy-start.1
  2.2 0.8 copy-done.1
  2.9 0.0 copy-start.2
  2.9 0.8 copy-done.2
  3.7 0.0 copy-start.3
  3.7 0.8 copy-done.3
  4.5 0.0 copy-start.4
  4.5 0.8 copy-done.4
  5.2 0.0 copy-start.5
  5.2 0.7 copy-done.5
  6.0 0.0 copy-start.6
  6.0 0.7 copy-done.6
  6.7 86.7 %shard_map.157 = (f32[3,8,192]{2,1,0:T(8,128)S(1)}, f32[3,8,192]{2,1,0:T(8,128)S(1)}, f32[3,8,192]{2,1,0:T(8,128)S(1)}) custom-call(f32[3,8,192]{2,1,0:T(8,128)S(1)} %bitcast.11, f32[3,8,192]{2,1,0:T(8,128)S(1)} %bitcast.12, f32[8]{0:T(128)S(1)} %copy-done.8, s32[8]{0:T(128)S(1)} %copy-done.9, s32[8]{0:T(128)S(1)} %copy-done.10, ...), custom_call_target="tpu_custom_call" | custom-call | tf_op jit(solution)/shard_map/pallas_call | solution.py:423
  93.4 0.6 copy.20
  94.0 0.6 copy.21
  94.6 0.6 copy.22
Async XLA Ops:
  0.6 0.7 copy-start.7
  0.6 0.7 copy-start.11
  0.7 0.7 copy-start.12
  0.7 0.7 copy-start.13
  0.7 0.7 copy-start.8
  0.7 0.7 copy-start.9
  0.7 0.7 copy-start.10
  1.4 0.8 copy-start
  2.2 0.8 copy-start.1
  2.9 0.8 copy-start.2
  3.7 0.8 copy-start.3
  4.5 0.8 copy-start.4
  5.2 0.7 copy-start.5
  6.0 0.7 copy-start.6

commit v4 on v2

--- a/solution.py
+++ b/solution.py
@@ -159,10 +159,11 @@
     side = jnp.where(lax.broadcasted_iota(jnp.int32, (1, LANES), 1) < NA, 14.0 * LOG2E, -14.0 * LOG2E).astype(F32)
     member_row = lax.broadcasted_iota(jnp.int32, (group, 1), 0)
     replica_row = lax.broadcasted_iota(jnp.int32, (replicas, 1), 0)
-    diagonal = (
-        lax.broadcasted_iota(jnp.int32, (group, LANES), 0)
+    diagonals = [
+        lax.broadcasted_iota(jnp.int32, (group, LANES), 0) + p * group
         == lax.broadcasted_iota(jnp.int32, (group, LANES), 1)
-    )
+        for p in range(parts)
+    ]
     target = jnp.zeros((replicas, 1), F32)
     source = jnp.zeros((replicas, 1), jnp.int32)
     for r in range(replicas):
@@ -286,7 +287,7 @@
         for c in order[2:]:
             forces[c] = force(p, c, sources[c - 1], sources[c], sources[c + 1])
         for copy in s_copies(t, p):
-            copy.wait()
+            copy.wait_recv()
         sources[-1] = s_recv[t, p, 0, :, NA:2 * NA]
         sources[cells] = s_recv[t, p, 1, :, 0:NA]
         for c in order[:2]:
@@ -300,29 +301,34 @@
             kinetic = kinetic + jnp.sum(v * v, axis=1, keepdims=True)
             state_v[p, d, :, 0:own] = v
             state_g[p, d, :, 0:own] = g
-        across = jnp.sum(jnp.where(diagonal, kinetic, 0.0), axis=0, keepdims=True)
-        kin_send[t, p] = across
-        kin_recv[t, p, n - 1] = across
+        for copy in vg_copies(t, p):
+            copy.start()
+        return jnp.sum(jnp.where(diagonals[p], kinetic, 0.0), axis=0, keepdims=True)
+
+    def spread_kinetic(t, across):
+        kin_send[t] = across
+        kin_recv[t, n - 1] = across
 
         def spread(d, inner):
             remote(
-                kin_send.at[t, p], kin_recv.at[t, p, d - 1], kin_send_sem.at[t, p],
-                kin_recv_sem.at[t, p], lax.rem(me + d, n),
+                kin_send.at[t], kin_recv.at[t, d - 1], kin_send_sem.at[t], kin_recv_sem.at[t],
+                lax.rem(me + d, n),
             ).start()
             return inner
 
         lax.fori_loop(1, n, spread, 0)
+
+    def wait_kinetic(t, sem):
+        everything = kin_recv.at[t, pl.ds(0, n - 1)]
+        pltpu.make_async_copy(everything, everything, sem.at[t]).wait()
+
+    def finish(t, p):
+        if p == 0:
+            wait_kinetic(t, kin_recv_sem)
         for copy in vg_copies(t, p):
-            copy.start()
-
-    def finish(t, p):
-        everything = kin_recv.at[t, p, pl.ds(0, n - 1)]
-        for copy in vg_copies(t, p):
-            copy.wait()
-        pltpu.make_async_copy(everything, everything, kin_send_sem.at[t, p]).wait()
-        pltpu.make_async_copy(everything, everything, kin_recv_sem.at[t, p]).wait()
-        collected = jnp.sum(kin_recv[t, p], axis=0)
-        gathered = jnp.sum(jnp.where(diagonal, collected, 0.0), axis=1, keepdims=True)
+            copy.wait_recv()
+        collected = jnp.sum(kin_recv[t], axis=0)
+        gathered = jnp.sum(jnp.where(diagonals[p], collected, 0.0), axis=1, keepdims=True)
         goal = target[p * group:(p + 1) * group]
         stretch = jnp.sqrt(goal / (gathered / (3.0 * own * n) + motion_work_lower_limit))
         stretch = jnp.where(t > 0, stretch, 1.0)
@@ -340,13 +346,21 @@
         for p in range(parts):
             pl.when(t > 0)(functools.partial(finish, t - 1, p))
             sources.append(first_half(t, p))
-        for p in range(parts):
-            second_half(t, p, sources[p])
+        spread_kinetic(t, sum(second_half(t, p, sources[p]) for p in range(parts)))
         return carry
 
     lax.fori_loop(0, STEPS + 1, step, 0)
     for p in range(parts):
         finish(STEPS, p)
+
+    def drain(t, carry):
+        wait_kinetic(t, kin_send_sem)
+        for p in range(parts):
+            for copy in s_copies(t, p) + vg_copies(t, p):
+                copy.wait_send()
+        return carry
+
+    lax.fori_loop(0, STEPS + 1, drain, 0)
 
     def pick(values):
         result = jnp.zeros_like(values)
@@ -423,16 +437,16 @@
             pltpu.VMEM((rounds, parts, 2, group, LANES), F32),
             pltpu.VMEM((rounds, parts, 2, 3, group, LANES), F32),
             pltpu.VMEM((rounds, parts, 2, 3, group, LANES), F32),
-            pltpu.VMEM((rounds, parts, 1, LANES), F32),
-            pltpu.VMEM((rounds, parts, n, 1, LANES), F32),
+            pltpu.VMEM((rounds, 1, LANES), F32),
+            pltpu.VMEM((rounds, n, 1, LANES), F32),
             pltpu.SemaphoreType.DMA((4,)),
             pltpu.SemaphoreType.DMA((4,)),
             pltpu.SemaphoreType.DMA((rounds, parts, 2)),
             pltpu.SemaphoreType.DMA((rounds, parts, 2)),
             pltpu.SemaphoreType.DMA((rounds, parts, 2)),
             pltpu.SemaphoreType.DMA((rounds, parts, 2)),
-            pltpu.SemaphoreType.DMA((rounds, parts)),
-            pltpu.SemaphoreType.DMA((rounds, parts)),
+            pltpu.SemaphoreType.DMA((rounds,)),
+            pltpu.SemaphoreType.DMA((rounds,)),
         ],
         compiler_params=pltpu.CompilerParams(
             collective_id=0, has_side_effects=True, vmem_limit_bytes=48 * 1024 * 1024

time: 80.3 us -> 88.3 us (1.100)
  Pallas kernels: 71.1 us -> 79.1 us
    pallas_call x1, Pallas kernels: 71.1 us -> 79.1 us  [on_device(): pl.pallas_call(functools.partial(kernel, n, replicas, cells, parts), out_...]
where the time goes in v4:
time: 88.3 us; the launch traced here: 87.7 us
  Pallas kernels  79.1 us (90%)
  local copies, waits for them, and re-layouts  7.82 us (9%)
    pallas_call x1, Pallas kernels, on_device(): pl.pallas_call(functools.partial(kernel, n, replicas, cells, parts), out_...  79.1 us
    unnamed x31, local copies, waits for them, and re-layouts  7.82 us

profile of v4, /device:TPU:0, one launch (start us, length us, event | category | flops | bytes accessed | tf_op | source)
XLA Modules:
  0.0 87.7 jit_solution(12129413641657677422)
XLA Ops:
  0.6 0.0 copy-start.7
  0.6 0.0 copy-start.11
  0.7 0.0 copy-start.12
  0.7 0.0 copy-start.13
  0.7 0.0 copy-start.8
  0.7 0.0 copy-start.9
  0.7 0.0 copy-start.10
  0.7 0.6 copy-done.7
  1.3 0.0 copy-done.11
  1.3 0.0 copy-done.12
  1.3 0.0 copy-done.13
  1.3 0.0 copy-done.8
  1.4 0.0 copy-done.9
  1.4 0.0 copy-done.10
  1.4 0.0 copy-start
  1.4 0.8 copy-done
  2.2 0.0 copy-start.1
  2.2 0.8 copy-done.1
  2.9 0.0 copy-start.2
  2.9 0.8 copy-done.2
  3.7 0.0 copy-start.3
  3.7 0.8 copy-done.3
  4.5 0.0 copy-start.4
  4.5 0.8 copy-done.4
  5.2 0.0 copy-start.5
  5.2 0.7 copy-done.5
  6.0 0.0 copy-start.6
  6.0 0.7 copy-done.6
  6.7 79.1 %shard_map.157 = (f32[3,8,192]{2,1,0:T(8,128)S(1)}, f32[3,8,192]{2,1,0:T(8,128)S(1)}, f32[3,8,192]{2,1,0:T(8,128)S(1)}) custom-call(f32[3,8,192]{2,1,0:T(8,128)S(1)} %bitcast.11, f32[3,8,192]{2,1,0:T(8,128)S(1)} %bitcast.12, f32[8]{0:T(128)S(1)} %copy-done.8, s32[8]{0:T(128)S(1)} %copy-done.9, s32[8]{0:T(128)S(1)} %copy-done.10, ...), custom_call_target="tpu_custom_call" | custom-call | tf_op jit(solution)/shard_map/pallas_call | solution.py:418
  85.8 0.6 copy.20
  86.4 0.6 copy.21
  87.1 0.6 copy.22
Async XLA Ops:
  0.6 0.7 copy-start.7
  0.6 0.7 copy-start.11
  0.7 0.7 copy-start.12
  0.7 0.7 copy-start.13
  0.7 0.7 copy-start.8
  0.7 0.7 copy-start.9
  0.7 0.7 copy-start.10
  1.4 0.8 copy-start
  2.2 0.8 copy-start.1
  2.9 0.8 copy-start.2
  3.7 0.8 copy-start.3
  4.5 0.8 copy-start.4
  5.2 0.7 copy-start.5
  6.0 0.7 copy-start.6
